TPU v7x, 32 devices: a whole 2x2x4 slice. The times are simulated.
32 devices in a mesh: vocab: 4 (over z), expert: 8 (over y, x, core).
Axes of the slice: x: 2, y: 2, z: 4, core: 2. Of those that a mesh axis runs over, the one named last changes fastest.
Arguments:
- token_ids: int32 [1024], replicated, may hold values from 0 to 75967
- word_mask: int32 [75968], P('vocab'), may hold values 0 or 1
- embed_table: bfloat16 [75968, 4096], P('vocab', 'expert'), may hold values from -6 to 6
- attn_out: bfloat16 [1024, 4096], P('expert', 'vocab'), may hold values from -6 to 6
- in_gain: float32 [4096], replicated, may hold values from 0.25 to 1.75
- key_weight: bfloat16 [4096, 512], P(None, 'vocab'), may hold values from -0.09375 to 0.09375
- key_gain: float32 [128], replicated, may hold values from 0.25 to 1.75
- post_gain: float32 [4096], replicated, may hold values from 0.25 to 1.75
- routes: int32 [1024, 8], P('expert'), may hold values from 0 to 15, all different within a row; in each aligned block of 128 rows (0 to 127, 128 to 255, ...) at most 96 rows name the same one
- gate_ints: int32 [1024, 8], P('expert'), may hold values from 1 to 63
- w_gate: bfloat16 [32, 4096, 768], P(('expert', 'vocab')), may hold values from -0.09375 to 0.09375
- w_up: bfloat16 [32, 4096, 768], P(('expert', 'vocab')), may hold values from -0.09375 to 0.09375
- w_down: bfloat16 [32, 768, 4096], P(('expert', 'vocab')), may hold values from -0.15625 to 0.15625
Outputs:
- expert_out: bfloat16 [1024, 4096], P('expert', 'vocab')
- key_heads: bfloat16 [1024, 512], P('expert', 'vocab')
Inputs may be any that keep to these rules, and one draw needn't show every extreme that they name: `routes`: each row names 8 different experts; within the 128 rows of one index of expert no expert is named by more than 96 rows, and in some such blocks one is named by exactly 96.
All inputs are finite; a program needn't handle non-finite values. No bound on the sum of `word_mask` on one device may be relied on, other than what follows from the above.
Results may differ from a plain program's by a relative error of at most 0.008.
Values may be sent and summed in bfloat16 or wider, within the bound.
A program may use at most 192 MiB of HBM per device.

v0:
```python
import jax
import jax.numpy as jnp
from jax import lax
from jax.sharding import PartitionSpec as P


def rms_rows(values, scale_gain):
    inverse_rms = lax.rsqrt(jnp.mean(values * values, axis=-1, keepdims=True) + 1e-06)
    return values * inverse_rms * scale_gain


def expert_apply(row_block, post_gain, gate_mat, up_mat, down_mat):
    normed = rms_rows(row_block.astype(jnp.float32), post_gain).astype(jnp.bfloat16)
    gate_val = jnp.dot(normed, gate_mat, preferred_element_type=jnp.float32)
    up_val = jnp.dot(normed, up_mat, preferred_element_type=jnp.float32)
    hidden = (jax.nn.silu(gate_val) * up_val).astype(jnp.bfloat16)
    return jnp.dot(hidden, down_mat, preferred_element_type=jnp.float32)


def on_device(
    token_ids,
    word_mask,
    embed_table,
    attn_out,
    in_gain,
    key_weight,
    key_gain,
    post_gain,
    routes,
    gate_ints,
    w_gate,
    w_up,
    w_down,
):
    n_vocab = lax.axis_size("vocab")
    n_expert = lax.axis_size("expert")
    vocab_rows = embed_table.shape[0]
    tok_dev = attn_out.shape[0]
    quarter = attn_out.shape[1]
    model_width = quarter * n_vocab
    top_count = routes.shape[1]
    experts_total = n_expert * n_vocab // 2
    capacity = tok_dev * top_count * 3 // (2 * experts_total)
    first_id = lax.axis_index("vocab") * vocab_rows
    local_ids = token_ids - first_id
    inside = (local_ids >= 0) & (local_ids < vocab_rows)
    safe_ids = jnp.clip(local_ids, 0, vocab_rows - 1)
    keep_row = inside & (word_mask[safe_ids] == 1)
    partial_value = jnp.where(
        keep_row[:, None], embed_table[safe_ids], jnp.zeros_like(embed_table[:1])
    )
    moved_rows = lax.all_to_all(partial_value, "expert", split_axis=0, concat_axis=1, tiled=True)
    summed = lax.psum_scatter(
        moved_rows.astype(jnp.float32).astype(jnp.bfloat16),
        "vocab",
        scatter_dimension=1,
        tiled=True,
    )
    full_rows = lax.all_gather(summed, "vocab", axis=1, tiled=True)
    normed_rows = rms_rows(full_rows.astype(jnp.float32), in_gain).astype(jnp.bfloat16)
    raw_keys = jnp.dot(normed_rows, key_weight, preferred_element_type=jnp.float32)
    key_heads = rms_rows(raw_keys, key_gain).astype(jnp.bfloat16)
    mid_quarter = (summed.astype(jnp.float32) + attn_out.astype(jnp.float32)).astype(jnp.bfloat16)
    flat_routes = routes.reshape(-1)
    onehot = (flat_routes[:, None] == jnp.arange(experts_total, dtype=jnp.int32)[None, :]).astype(
        jnp.int32
    )
    slot_rank = jnp.sum((jnp.cumsum(onehot, axis=0) - onehot) * onehot, axis=1)
    token_of = jnp.arange(tok_dev * top_count, dtype=jnp.int32) // top_count
    slot_token = (
        jnp.full((experts_total * capacity,), tok_dev, jnp.int32)
        .at[flat_routes * capacity + slot_rank]
        .set(token_of)
    )
    padded = jnp.concatenate([mid_quarter, jnp.zeros((1, quarter), jnp.bfloat16)], axis=0)
    send_rows = padded[slot_token]
    gate_share = gate_ints.astype(jnp.float32) / jnp.sum(gate_ints, axis=1, keepdims=True).astype(
        jnp.float32
    )
    doubled = jnp.broadcast_to(
        send_rows.reshape(experts_total, 1, capacity, quarter),
        (experts_total, 2, capacity, quarter),
    ).reshape(2 * experts_total, capacity, quarter)
    arrived = lax.all_to_all(doubled, ("expert", "vocab"), split_axis=0, concat_axis=2, tiled=True)
    outputs = expert_apply(
        arrived.reshape(capacity * n_expert, model_width), post_gain, w_gate[0], w_up[0], w_down[0]
    )
    returned = lax.all_to_all(
        outputs.reshape(capacity, 2 * experts_total, quarter),
        ("expert", "vocab"),
        split_axis=1,
        concat_axis=1,
        tiled=True,
    )
    half_sum = jnp.sum(returned.reshape(capacity, experts_total, 2, quarter), axis=2)
    rounded = lax.optimization_barrier(half_sum.astype(jnp.bfloat16))
    combined = rounded.astype(jnp.float32).reshape(capacity * experts_total, quarter)
    slot_index = slot_rank * experts_total + flat_routes
    picked = combined[slot_index].reshape(tok_dev, top_count, quarter)
    weighted = jnp.sum(picked * gate_share[:, :, None], axis=1)
    return (weighted.astype(jnp.bfloat16), key_heads)


def solution(mesh):
    return jax.shard_map(
        on_device,
        mesh=mesh,
        in_specs=(
            P(),
            P("vocab"),
            P("vocab", "expert"),
            P("expert", "vocab"),
            P(),
            P(None, "vocab"),
            P(),
            P(),
            P("expert", None),
            P("expert", None),
            P(("expert", "vocab"), None, None),
            P(("expert", "vocab"), None, None),
            P(("expert", "vocab"), None, None),
        ),
        out_specs=(P("expert", "vocab"), P("expert", "vocab")),
        check_vma=False,
    )
```

profile of v0, /device:TPU:8, one launch (start us, length us, event | category | flops | bytes accessed | tf_op | source)
XLA Modules:
  0.0 643.4 jit_solution(3366588678373440411)
XLA Ops:
  8.0 5.9 gather_fusion
  14.6 13.0 %gather_fusion.1 = bf16[1024,512]{1,0:T(8,128)(2,1)S(1)} fusion(bf16[18992,512]{1,0:T(8,128)(2,1)} %param.15, s32[1024]{0:T(1024)S(1)} %fusion.27), kind=kCustom, calls=%fused_computation.1 | custom fusion | bytes 2101248 | tf_op jit(solution)/shard_map/gather | solution.py:50
  27.9 18.9 %all_to_all.30 = bf16[8,128,512]{2,1,0:T(8,128)(2,1)S(1)} all-to-all(bf16[8,128,512]{2,1,0:T(8,128)(2,1)S(1)} %broadcast_select_fusion), channel_id=1, replica_groups=mesh['vocab'=4,'expert'=8] {'expert'}, dimensions={0} | all-to-all | bytes 2097152 | tf_op jit(solution)/shard_map/all_to_all | solution.py:52
  48.3 4.5 reduce-window.6
  53.3 4.3 scatter_custom_fusion
  57.7 14.8 %reduce-scatter.2.cloned.1.call-done = bf16[128,1024]{1,0:T(8,128)(2,1)} async-done(((bf16[128,4096]{1,0:T(8,128)(2,1)}), bf16[128,1024]{1,0:T(8,128)(2,1)}) %reduce-scatter.2.cloned.1.call-update) | async-done | bytes 262160 | tf_op jit(solution)/shard_map/reduce_scatter | solution.py:53
  73.5 5.9 gather_fusion.2
  79.4 5.6 broadcast_in_dim.56
  85.0 6.6 %all-to-all-start.1 = ((bf16[32,96,1024]{2,1,0:T(8,128)(2,1)}), bf16[32,96,1024]{2,1,0:T(8,128)(2,1)}, u32[]{:S(2)}, u32[]{:S(2)}) async-start(bf16[32,96,1024]{2,1,0:T(8,128)(2,1)} %bitcast.72), calls=%async_computation.2 | async-start | bytes 12582912 | tf_op jit(solution)/shard_map/all_to_all | solution.py:84
  91.7 139.1 %all-to-all-done.1 = bf16[32,96,1024]{2,1,0:T(8,128)(2,1)} async-done(((bf16[32,96,1024]{2,1,0:T(8,128)(2,1)}), bf16[32,96,1024]{2,1,0:T(8,128)(2,1)}, u32[]{:S(2)}, u32[]{:S(2)}) %all-to-all-start.1) | async-done | bytes 6291488 | tf_op jit(solution)/shard_map/all_to_all | solution.py:84
  235.6 4.3 fusion.4
  239.9 6.2 copy.59
  246.1 10.8 %convert_element_type.76 = bf16[768,4096]{1,0:T(8,128)(2,1)} reshape(bf16[1,96,32,1024]{3,2,1,0:T(8,128)(2,1)} %copy.59) | data formatting | bytes 12582912 | tf_op jit(solution)/shard_map/convert_element_type | solution.py:13
  256.9 9.3 %fusion.9 = f32[768,768]{1,0:T(8,128)S(1)} fusion(bf16[768,4096]{1,0:T(8,128)(2,1)} %convert_element_type.76, bf16[1,4096,768]{2,1,0:T(8,128)(2,1)} %param.23), kind=kOutput, calls=%fused_computation.16 | convolution fusion | flops 4831838208 | bytes 14942208 | tf_op jit(solution)/shard_map/dot_general | solution.py:14
  266.2 8.0 %multiply_convert_fusion = bf16[768,768]{1,0:T(8,128)(2,1)S(1)} fusion(f32[768,768]{1,0:T(8,128)S(1)} %fusion.9, bf16[768,4096]{1,0:T(8,128)(2,1)S(1)} %copy-done.1, bf16[1,4096,768]{2,1,0:T(8,128)(2,1)} %param.24), kind=kOutput, calls=%fused_computation.22 | convolution fusion | flops 4835377152 | bytes 16121856 | tf_op jit(solution)/shard_map/dot_general | solution.py:15
  274.2 10.7 %fusion.5 = f32[768,4096]{1,0:T(8,128)} fusion(bf16[768,768]{1,0:T(8,128)(2,1)S(1)} %multiply_convert_fusion, bf16[1,768,4096]{2,1,0:T(8,128)(2,1)} %param.25), kind=kOutput, calls=%fused_computation.12 | convolution fusion | flops 4831838208 | bytes 20054016 | tf_op jit(solution)/shard_map/dot_general | solution.py:17
  284.9 14.6 %reshape.177 = f32[96,32,1024]{2,1,0:T(8,128)} reshape(f32[768,4096]{1,0:T(8,128)} %fusion.5) | data formatting | bytes 25165824 | tf_op jit(solution)/shard_map/reshape | solution.py:89
  299.5 16.4 %copy.60 = f32[96,32,1024]{2,0,1:T(8,128)} copy(f32[96,32,1024]{2,1,0:T(8,128)} %reshape.177) | data formatting | bytes 25165824 | tf_op jit(solution)/shard_map/reshape | solution.py:89
  316.0 4.7 all-to-all-start.2
  321.6 79.7 %all-gather.2.cloned.1.call-done = bf16[128,4096]{1,0:T(8,128)(2,1)} async-done(((bf16[128,1024]{1,0:T(8,128)(2,1)}), bf16[128,4096]{1,0:T(8,128)(2,1)}) %all-gather.2.cloned.1.call-update) | async-done | bytes 1048592 | tf_op jit(solution)/shard_map/all_gather | solution.py:59
  405.5 206.5 %all-to-all-done.2 = f32[96,32,1024]{2,0,1:T(8,128)} async-done(((f32[96,32,1024]{2,0,1:T(8,128)}), f32[96,32,1024]{2,0,1:T(8,128)}, u32[]{:S(2)}, u32[]{:S(2)}) %all-to-all-start.2) | async-done | bytes 12582944 | tf_op jit(solution)/shard_map/all_to_all | solution.py:88
  612.0 6.5 %bitcast_reduce_fusion = bf16[96,16,1024]{2,0,1:T(8,128)(2,1)S(1)} fusion(f32[96,32,1024]{2,0,1:T(8,128)} %all-to-all-done.2), kind=kLoop, calls=%fused_computation.5 | loop fusion | flops 1572864 | bytes 15728640 | tf_op jit(solution)/shard_map/reduce_sum | solution.py:95
  618.5 4.5 copy.61
  622.9 9.2 %gather_fusion.3 = f32[1024,1024]{1,0:T(8,128)} fusion(f32[1536,1024]{1,0:T(8,128)} %bitcast.71, s32[1024]{0:T(1024)S(1)} %broadcast_clamp_fusion), kind=kCustom, calls=%fused_computation.3 | custom fusion | bytes 8392704 | tf_op jit(solution)/shard_map/gather | solution.py:99
  (65 shorter events, 18.8 us)
Async XLA Ops:
  7.2 395.6 %copy-start = (bf16[4096,128]{1,0:T(8,128)(2,1)S(1)}, bf16[4096,128]{1,0:T(8,128)(2,1)}, u32[]{:S(2)}) copy-start(bf16[4096,128]{1,0:T(8,128)(2,1)} %param.18) | copy-start | bytes 3145732
  7.2 65.3 %reduce-scatter.2.cloned.1.call-start = ((), (), s32[]{:S(2)}) async-start(), calls=%async_computation.4 | async-start | bytes 1310720 | tf_op jit(solution)/shard_map/reduce_scatter | solution.py:53
  14.6 33.3 %copy-start.5 = (s32[128,8]{0,1:T(8,128)S(1)}, s32[128,8]{0,1:T(8,128)}, u32[]{:S(2)}) copy-start(s32[128,8]{0,1:T(8,128)} %param.21) | copy-start | bytes 12292
  27.7 44.8 %copy-start.2 = (bf16[128,1024]{1,0:T(8,128)(2,1)S(1)}, bf16[128,1024]{1,0:T(8,128)(2,1)}, u32[]{:S(2)}) copy-start(bf16[128,1024]{1,0:T(8,128)(2,1)} %param.16) | copy-start | bytes 786436
  85.0 6.6 %copy-start.4 = (f32[4096]{0:T(1024)S(1)}, f32[4096]{0:T(1024)}, u32[]{:S(2)}) copy-start(f32[4096]{0:T(1024)} %param.20) | copy-start | bytes 49156
  85.0 145.8 %all-to-all-start.1 = ((bf16[32,96,1024]{2,1,0:T(8,128)(2,1)}), bf16[32,96,1024]{2,1,0:T(8,128)(2,1)}, u32[]{:S(2)}, u32[]{:S(2)}) async-start(bf16[32,96,1024]{2,1,0:T(8,128)(2,1)} %bitcast.72), calls=%async_computation.2 | async-start | bytes 12582912 | tf_op jit(solution)/shard_map/all_to_all | solution.py:84
  256.9 9.3 %copy-start.1 = (bf16[768,4096]{1,0:T(8,128)(2,1)S(1)}, bf16[768,4096]{1,0:T(8,128)(2,1)}, u32[]{:S(2)}) copy-start(bf16[768,4096]{1,0:T(8,128)(2,1)} %convert_element_type.76) | copy-start | bytes 18874372
  316.0 5.5 copy-start.3
  316.0 86.8 %copy-start.7 = (f32[4096]{0:T(1024)S(1)}, f32[4096]{0:T(1024)}, u32[]{:S(2)}) copy-start(f32[4096]{0:T(1024)} %param.17) | copy-start | bytes 49156
  316.0 88.7 %copy-start.6 = (f32[128]{0:T(128)S(1)}, f32[128]{0:T(128)}, u32[]{:S(2)}) copy-start(f32[128]{0:T(128)} %param.19) | copy-start | bytes 1540
  316.0 296.0 %all-to-all-start.2 = ((f32[96,32,1024]{2,0,1:T(8,128)}), f32[96,32,1024]{2,0,1:T(8,128)}, u32[]{:S(2)}, u32[]{:S(2)}) async-start(f32[96,32,1024]{2,0,1:T(8,128)} %copy.60), calls=%async_computation.3 | async-start | bytes 25165824 | tf_op jit(solution)/shard_map/all_to_all | solution.py:88
  320.7 80.6 %all-gather.2.cloned.1.call-start = ((), (), s32[]{:S(2)}) async-start(), calls=%async_computation.5 | async-start | bytes 1310720 | tf_op jit(solution)/shard_map/all_gather | solution.py:59
Sparse Core Ops, SparseCore 0:
  48.0 24.4 reduce-scatter.1
  323.2 78.0 all-gather.1
where the time goes:
time: 652 us; the launch traced here: 643 us
  waiting for transfers between devices  441 us (68%)
  local copies, waits for them, and re-layouts  99.6 us (15%)
  matrix products  29.9 us (5%)
  other arithmetic  28.3 us (4%)
  blocking collectives  18.9 us (3%)
  between operations  14.6 us (2%)
  starting transfers between devices  11.6 us (2%)
    all_to_all x1, waiting for transfers between devices, on_device(): lax.all_to_all(outputs.reshape(capacity, 2 * experts_total, quarter), ('e...  206 us
    all_to_all x1, waiting for transfers between devices, on_device(): lax.all_to_all(doubled, ('expert', 'vocab'), split_axis=0, concat_axis=2,...  139 us
    all_gather x1, waiting for transfers between devices, on_device(): full_rows = lax.all_gather(summed, 'vocab', axis=1, tiled=True)  79.7 us
    reshape x2, local copies, waits for them, and re-layouts, on_device(): outputs.reshape(capacity, 2 * experts_total, quarter)  31 us
    all_to_all x1, blocking collectives, on_device(): lax.all_to_all(partial_value, 'expert', split_axis=0, concat_axis=1, tile...  18.9 us
    convert_element_type x2, local copies, waits for them, and re-layouts, expert_apply(): rms_rows(row_block.astype(jnp.float32), post_gain).astype(jnp.bfloat16)  17 us
    reduce_scatter x1, waiting for transfers between devices, on_device(): lax.psum_scatter(moved_rows.astype(jnp.float32).astype(jnp.bfloat16), 'vo...  14.8 us
  transfers between devices with their start and end apart: 4, of which 4 were waited for; matrix products, arithmetic and copies ran while one was open for 2% of the time, Pallas kernels for 0%

commit v1 on v0

v1 whole, which is shorter than its diff:
```python
import jax
import jax.numpy as jnp
from jax import lax
from jax.sharding import PartitionSpec as P


def rms_rows(values, scale_gain):
    inverse_rms = lax.rsqrt(jnp.mean(values * values, axis=-1, keepdims=True) + 1e-06)
    return values * inverse_rms * scale_gain


def on_device(
    token_ids,
    word_mask,
    embed_table,
    attn_out,
    in_gain,
    key_weight,
    key_gain,
    post_gain,
    routes,
    gate_ints,
    w_gate,
    w_up,
    w_down,
):
    n_vocab = lax.axis_size("vocab")
    n_expert = lax.axis_size("expert")
    vocab_rows = embed_table.shape[0]
    experts_total = n_expert * n_vocab // 2
    whole_mesh = ("expert", "vocab")
    my_vocab = lax.axis_index("vocab")
    my_expert = (lax.axis_index("expert") * n_vocab + my_vocab) // 2

    gate_share = gate_ints.astype(jnp.float32) / jnp.sum(gate_ints, axis=1, keepdims=True).astype(
        jnp.float32
    )
    onehot = routes[:, :, None] == jnp.arange(experts_total, dtype=jnp.int32)[None, None, :]
    share_of = jnp.sum(jnp.where(onehot, gate_share[:, :, None], 0.0), axis=1)
    all_shares = lax.all_gather(share_of, "expert", axis=0, tiled=True)
    my_share = lax.dynamic_slice_in_dim(all_shares, my_expert, 1, axis=1)

    attn_rows = lax.all_to_all(attn_out, "vocab", split_axis=0, concat_axis=1, tiled=True)

    local_ids = token_ids - my_vocab * vocab_rows
    inside = (local_ids >= 0) & (local_ids < vocab_rows)
    safe_ids = jnp.clip(local_ids, 0, vocab_rows - 1)
    keep_row = inside & (word_mask[safe_ids] == 1)
    partial_value = jnp.where(
        keep_row[:, None], embed_table[safe_ids], jnp.zeros_like(embed_table[:1])
    )
    moved_rows = lax.all_to_all(partial_value, "expert", split_axis=0, concat_axis=1, tiled=True)
    rows = lax.psum_scatter(moved_rows, "vocab", scatter_dimension=0, tiled=True)
    rows = rows.astype(jnp.float32)

    mid_rows = (rows + attn_rows.astype(jnp.float32)).astype(jnp.bfloat16)
    expert_in = rms_rows(mid_rows.astype(jnp.float32), post_gain).astype(jnp.bfloat16)
    tokens_in = lax.all_gather(expert_in, whole_mesh, axis=0, tiled=True)

    normed_rows = rms_rows(rows, in_gain).astype(jnp.bfloat16)
    key_rows = lax.all_gather(normed_rows, "vocab", axis=0, tiled=True)
    raw_keys = jnp.dot(key_rows, key_weight, preferred_element_type=jnp.float32)
    key_heads = rms_rows(raw_keys, key_gain).astype(jnp.bfloat16)

    gate_val = jnp.dot(tokens_in, w_gate[0], preferred_element_type=jnp.float32)
    up_val = jnp.dot(tokens_in, w_up[0], preferred_element_type=jnp.float32)
    hidden = (jax.nn.silu(gate_val) * up_val).astype(jnp.bfloat16)
    parts = jnp.dot(hidden, w_down[0], preferred_element_type=jnp.float32)
    weighted = (parts * my_share).astype(jnp.bfloat16)
    by_tokens = lax.psum_scatter(weighted, "expert", scatter_dimension=0, tiled=True)
    expert_out = lax.psum_scatter(by_tokens, "vocab", scatter_dimension=1, tiled=True)
    return (expert_out, key_heads)


def solution(mesh):
    return jax.shard_map(
        on_device,
        mesh=mesh,
        in_specs=(
            P(),
            P("vocab"),
            P("vocab", "expert"),
            P("expert", "vocab"),
            P(),
            P(None, "vocab"),
            P(),
            P(),
            P("expert", None),
            P("expert", None),
            P(("expert", "vocab"), None, None),
            P(("expert", "vocab"), None, None),
            P(("expert", "vocab"), None, None),
        ),
        out_specs=(P("expert", "vocab"), P("expert", "vocab")),
        check_vma=False,
    )
```

time: 652 us -> 325 us (0.50)
  waiting for transfers between devices: 441 us -> 204 us
  local copies, waits for them, and re-layouts: 99.6 us -> 21.7 us
  blocking collectives: 18.9 us -> 45 us
  other arithmetic: 28.3 us -> 4.83 us
  starting transfers between devices: 11.6 us -> 0.2 us
    all_to_all x2 -> x0, waiting for transfers between devices: 346 us -> none  [the longest x1 206 us: on_device(): lax.all_to_all(outputs.reshape(capacity, 2 * experts_total, quarter), ('e...]
    reduce_scatter x1 -> x3, waiting for transfers between devices: 14.8 us -> 107 us  [the longest x1 69.4 us: on_device(): lax.psum_scatter(weighted, 'expert', scatter_dimension=0, tiled=True)]
    reshape x4 -> x0, local copies, waits for them, and re-layouts: 35.6 us -> none  [the longest x2 31 us: on_device(): outputs.reshape(capacity, 2 * experts_total, quarter)]
    all_to_all x0 -> x1, blocking collectives: none -> 17 us  [on_device(): lax.all_to_all(attn_out, 'vocab', split_axis=0, concat_axis=1, tiled=True)]
    convert_element_type x2 -> x1, local copies, waits for them, and re-layouts: 17 us -> 0.04 us  [on_device(): mid_rows = (rows + attn_rows.astype(jnp.float32)).astype(jnp.bfloat16)]
    all_gather x1 -> x2, waiting for transfers between devices: 79.7 us -> 96.3 us  [the longest x1 67 us: on_device(): tokens_in = lax.all_gather(expert_in, whole_mesh, axis=0, tiled=True)]
    gather x2 -> x0, local copies, waits for them, and re-layouts: 15.1 us -> none  [the longest x1 9.24 us: on_device(): picked = combined[slot_index].reshape(tok_dev, top_count, quarter)]
    all_to_all x2 -> x0, starting transfers between devices: 11.3 us -> none  [the longest x1 6.59 us: on_device(): lax.all_to_all(doubled, ('expert', 'vocab'), split_axis=0, concat_axis=2,...]
  transfers between devices with their start and end apart: 4 -> 5, of which waited for: 4 -> 5; matrix products, arithmetic and copies ran while one was open for 2% -> 1% of each run, Pallas kernels for 0% -> 0%
where the time goes in v1:
time: 325 us; the launch traced here: 321 us
  waiting for transfers between devices  204 us (63%)
  blocking collectives  45 us (14%)
  matrix products  31.6 us (10%)
  local copies, waits for them, and re-layouts  21.7 us (7%)
  between operations  14 us (4%)
  other arithmetic  4.83 us (1%)
    reduce_scatter x1, waiting for transfers between devices, on_device(): lax.psum_scatter(weighted, 'expert', scatter_dimension=0, tiled=True)  69.4 us
    all_gather x1, waiting for transfers between devices, on_device(): tokens_in = lax.all_gather(expert_in, whole_mesh, axis=0, tiled=True)  67 us
    all_gather x1, waiting for transfers between devices, on_device(): key_rows = lax.all_gather(normed_rows, 'vocab', axis=0, tiled=True)  29.3 us
    reduce_scatter x1, waiting for transfers between devices, on_device(): lax.psum_scatter(by_tokens, 'vocab', scatter_dimension=1, tiled=True)  24.7 us
    all_to_all x1, blocking collectives, on_device(): lax.all_to_all(partial_value, 'expert', split_axis=0, concat_axis=1, tile...  18.9 us
    all_to_all x1, blocking collectives, on_device(): lax.all_to_all(attn_out, 'vocab', split_axis=0, concat_axis=1, tiled=True)  17 us
    gather x2, local copies, waits for them, and re-layouts, on_device(): embed_table[safe_ids]  13.7 us
    reduce_scatter x1, waiting for transfers between devices, on_device(): lax.psum_scatter(moved_rows, 'vocab', scatter_dimension=0, tiled=True)  12.6 us
  transfers between devices with their start and end apart: 5, of which 5 were waited for; matrix products, arithmetic and copies ran while one was open for 1% of the time, Pallas kernels for 0%

profile of v1, /device:TPU:8, one launch (start us, length us, event | category | flops | bytes accessed | tf_op | source)
XLA Modules:
  0.0 321.0 jit_solution(1872449881291243474)
XLA Ops:
  7.2 0.8 fusion.14
  8.0 5.9 %gather_fusion = s32[1024]{0:T(1024)S(1)} fusion(s32[18992]{0:T(1024)} %param.14, s32[1024]{0:T(1024)S(1)} %fusion.14), kind=kCustom, calls=%fused_computation | custom fusion | bytes 12288 | tf_op jit(solution)/shard_map/gather | solution.py:48
  13.9 0.7 and_bitcast_fusion
  14.6 13.0 %gather_fusion.1 = bf16[1024,512]{1,0:T(8,128)(2,1)S(1)} fusion(bf16[18992,512]{1,0:T(8,128)(2,1)} %param.15, s32[1024]{0:T(1024)S(1)} %fusion.14), kind=kCustom, calls=%fused_computation.1 | custom fusion | bytes 2101248 | tf_op jit(solution)/shard_map/gather | solution.py:50
  27.7 0.7 copy.30
  28.4 0.1 broadcast_select_fusion
  28.5 18.9 %all_to_all.29 = bf16[8,128,512]{1,2,0:T(8,128)(2,1)S(1)} all-to-all(bf16[8,128,512]{1,2,0:T(8,128)(2,1)S(1)} %broadcast_select_fusion), channel_id=1, replica_groups=mesh['vocab'=4,'expert'=8] {'expert'}, dimensions={0} | all-to-all | bytes 2097152 | tf_op jit(solution)/shard_map/all_to_all | solution.py:52
  47.4 1.3 copy.34
  48.7 17.0 %all_to_all.30 = bf16[4,32,1024]{2,1,0:T(8,128)(2,1)S(1)} all-to-all(bf16[4,32,1024]{2,1,0:T(8,128)(2,1)S(1)} %bitcast.33), channel_id=1, replica_groups=mesh['vocab'=4,'expert'=8] {'vocab'}, dimensions={0} | all-to-all | bytes 524288 | tf_op jit(solution)/shard_map/all_to_all | solution.py:43
  65.9 12.6 %reduce-scatter.10.cloned.1.call-done = bf16[32,4096]{1,0:T(8,128)(2,1)} async-done(((bf16[128,4096]{1,0:T(8,128)(2,1)}), bf16[32,4096]{1,0:T(8,128)(2,1)}) %reduce-scatter.10.cloned.1.call-update) | async-done | bytes 262160 | tf_op jit(solution)/shard_map/reduce_scatter | solution.py:53
  78.4 1.2 fusion.11
  79.6 1.9 fusion.13
  81.7 9.1 %all_gather.10 = f32[1024,16]{0,1:T(8,128)S(1)} all-gather(f32[128,16]{0,1:T(8,128)S(1)} %select_reduce_fusion), channel_id=1, replica_groups=mesh['vocab'=4,'expert'=8] {'expert'}, dimensions={0}, use_global_device_ids=true | all-gather | bytes 73728 | tf_op jit(solution)/shard_map/all_gather | solution.py:40
  90.8 67.0 %all-gather.3.cloned.1.call-done = bf16[1024,4096]{1,0:T(8,128)(2,1)} async-done(((bf16[32,4096]{1,0:T(8,128)(2,1)}), bf16[1024,4096]{1,0:T(8,128)(2,1)}) %all-gather.3.cloned.1.call-update) | async-done | bytes 8388624 | tf_op jit(solution)/shard_map/all_gather | solution.py:58
  157.8 11.0 %fusion.1 = f32[1024,768]{1,0:T(8,128)S(1)} fusion(bf16[1024,4096]{1,0:T(8,128)(2,1)} %all-gather.3.cloned.1.call-done, bf16[1,4096,768]{2,1,0:T(8,128)(2,1)} %param.24), kind=kOutput, calls=%fused_computation.4 | convolution fusion | flops 6442450944 | bytes 17825792 | tf_op jit(solution)/shard_map/dot_general | solution.py:66
  168.9 9.9 %multiply_convert_fusion.1 = bf16[1024,768]{1,0:T(8,128)(2,1)S(1)} fusion(f32[1024,768]{1,0:T(8,128)S(1)} %fusion.1, bf16[1024,4096]{1,0:T(8,128)(2,1)S(1)} %copy-done.7, bf16[1,4096,768]{2,1,0:T(8,128)(2,1)} %param.23), kind=kOutput, calls=%fused_computation.8 | convolution fusion | flops 6447169536 | bytes 19398656 | tf_op jit(solution)/shard_map/dot_general | solution.py:65
  178.9 8.9 %multiply_convert_fusion = bf16[1024,4096]{1,0:T(8,128)(2,1)} fusion(f32[1024]{0:T(1024)S(1)} %bitcast.34, bf16[1024,768]{1,0:T(8,128)(2,1)S(1)} %multiply_convert_fusion.1, bf16[1,768,4096]{2,1,0:T(8,128)(2,1)S(1)} %bitcast.36), kind=kOutput, calls=%fused_computation.2 | convolution fusion | flops 6450839552 | bytes 16257024 | tf_op jit(solution)/shard_map/dot_general | solution.py:68
  187.8 0.5 all-gather.5.cloned.1.call-update
  188.4 69.4 %reduce-scatter.6.cloned.1.call-done = bf16[128,4096]{1,0:T(8,128)(2,1)} async-done(((bf16[1024,4096]{1,0:T(8,128)(2,1)}), bf16[128,4096]{1,0:T(8,128)(2,1)}) %reduce-scatter.6.cloned.1.call-update) | async-done | bytes 1048592 | tf_op jit(solution)/shard_map/reduce_scatter | solution.py:70
  257.8 29.3 %all-gather.5.cloned.1.call-done = bf16[128,4096]{1,0:T(8,128)(2,1)} async-done(((bf16[32,4096]{1,0:T(8,128)(2,1)}), bf16[128,4096]{1,0:T(8,128)(2,1)}) %all-gather.5.cloned.1.call-update) | async-done | bytes 1048592 | tf_op jit(solution)/shard_map/all_gather | solution.py:61
  287.1 1.8 multiply_reduce_fusion
  288.9 0.1 multiply_convert_fusion.2
  289.0 0.7 copy.33
  289.7 24.7 %reduce-scatter.8.cloned.1.call-done = bf16[128,1024]{1,0:T(8,128)(2,1)} async-done(((bf16[128,4096]{1,0:T(8,128)(2,1)}), bf16[128,1024]{1,0:T(8,128)(2,1)}) %reduce-scatter.8.cloned.1.call-update) | async-done | bytes 262160 | tf_op jit(solution)/shard_map/reduce_scatter | solution.py:71
  (39 shorter events, 0.5 us)
Async XLA Ops:
  7.2 279.9 %copy-start = (bf16[4096,128]{1,0:T(8,128)(2,1)S(1)}, bf16[4096,128]{1,0:T(8,128)(2,1)}, u32[]{:S(2)}) copy-start(bf16[4096,128]{1,0:T(8,128)(2,1)} %param.18) | copy-start | bytes 3145732
  7.2 71.2 %reduce-scatter.10.cloned.1.call-start = ((), (), s32[]{:S(2)}) async-start(), calls=%async_computation.9 | async-start | bytes 1310720 | tf_op jit(solution)/shard_map/reduce_scatter | solution.py:53
  27.7 21.1 %copy-start.1 = (bf16[128,1024]{1,0:T(8,128)(2,1)S(1)}, bf16[128,1024]{1,0:T(8,128)(2,1)}, u32[]{:S(2)}) copy-start(bf16[128,1024]{1,0:T(8,128)(2,1)} %param.16) | copy-start | bytes 786436
  27.7 51.9 %copy-start.2 = (f32[4096]{0:T(1024)S(1)}, f32[4096]{0:T(1024)}, u32[]{:S(2)}) copy-start(f32[4096]{0:T(1024)} %param.17) | copy-start | bytes 49156
  27.7 51.9 %copy-start.3 = (f32[4096]{0:T(1024)S(1)}, f32[4096]{0:T(1024)}, u32[]{:S(2)}) copy-start(f32[4096]{0:T(1024)} %param.20) | copy-start | bytes 49156
  28.4 53.3 %copy-start.4 = (s32[128,8]{0,1:T(8,128)S(1)}, s32[128,8]{0,1:T(8,128)}, u32[]{:S(2)}) copy-start(s32[128,8]{0,1:T(8,128)} %param.22) | copy-start | bytes 12292
  28.4 53.3 %copy-start.5 = (s32[128,8]{0,1:T(8,128)S(1)}, s32[128,8]{0,1:T(8,128)}, u32[]{:S(2)}) copy-start(s32[128,8]{0,1:T(8,128)} %param.21) | copy-start | bytes 12292
  48.7 109.1 %all-gather.3.cloned.1.call-start = ((), (), s32[]{:S(2)}) async-start(), calls=%async_computation.5 | async-start | bytes 8650752 | tf_op jit(solution)/shard_map/all_gather | solution.py:58
  81.6 176.2 %reduce-scatter.6.cloned.1.call-start = ((), (), s32[]{:S(2)}) async-start(), calls=%async_computation.6 | async-start | bytes 9437184 | tf_op jit(solution)/shard_map/reduce_scatter | solution.py:70
  157.8 11.1 %copy-start.7 = (bf16[1024,4096]{1,0:T(8,128)(2,1)S(1)}, bf16[1024,4096]{1,0:T(8,128)(2,1)}, u32[]{:S(2)}) copy-start(bf16[1024,4096]{1,0:T(8,128)(2,1)} %all-gather.3.cloned.1.call-done) | copy-start | bytes 25165828
  157.8 21.0 %slice-start = ((s8[6291456]{0:T(1024)(128)(4,1)}), s8[4194304]{0:T(1024)(128)(4,1)S(1)}, s32[]{:S(2)}) async-start(s8[6291456]{0:T(1024)(128)(4,1)} %bitcast.35), calls=%async_computation.10 | async-start | bytes 8388608
  168.9 10.0 %slice-start.1 = ((s8[6291456]{0:T(1024)(128)(4,1)}), s8[2097152]{0:T(1024)(128)(4,1)S(1)}, s32[]{:S(2)}) async-start(s8[6291456]{0:T(1024)(128)(4,1)} %bitcast.35), calls=%async_computation.11 | async-start | bytes 4194304
  187.7 101.1 %copy-start.6 = (f32[128]{0:T(128)S(1)}, f32[128]{0:T(128)}, u32[]{:S(2)}) copy-start(f32[128]{0:T(128)} %param.19) | copy-start | bytes 1540
  187.8 99.3 %all-gather.5.cloned.1.call-start = ((), (), s32[]{:S(2)}) async-start(), calls=%async_computation.8 | async-start | bytes 1310720 | tf_op jit(solution)/shard_map/all_gather | solution.py:61
  188.3 126.1 %reduce-scatter.8.cloned.1.call-start = ((), (), s32[]{:S(2)}) async-start(), calls=%async_computation.7 | async-start | bytes 1310720 | tf_op jit(solution)/shard_map/reduce_scatter | solution.py:71
Sparse Core Ops, SparseCore 0:
  48.8 29.5 reduce-scatter.9
  82.3 75.4 all-gather.2
  187.9 69.8 reduce-scatter.5
  259.2 27.8 all-gather.4
  289.8 24.5 reduce-scatter.7

commit v2 on v1

--- a/solution.py
+++ b/solution.py
@@ -40,7 +40,9 @@
     all_shares = lax.all_gather(share_of, "expert", axis=0, tiled=True)
     my_share = lax.dynamic_slice_in_dim(all_shares, my_expert, 1, axis=1)
 
-    attn_rows = lax.all_to_all(attn_out, "vocab", split_axis=0, concat_axis=1, tiled=True)
+    own_rows = attn_out.shape[0] // n_vocab
+    attn_full = lax.all_gather(attn_out, "vocab", axis=1, tiled=True)
+    attn_rows = lax.dynamic_slice_in_dim(attn_full, my_vocab * own_rows, own_rows, axis=0)
 
     local_ids = token_ids - my_vocab * vocab_rows
     inside = (local_ids >= 0) & (local_ids < vocab_rows)
@@ -58,15 +60,16 @@
     tokens_in = lax.all_gather(expert_in, whole_mesh, axis=0, tiled=True)
 
     normed_rows = rms_rows(rows, in_gain).astype(jnp.bfloat16)
+    tokens_in, normed_rows = lax.optimization_barrier((tokens_in, normed_rows))
     key_rows = lax.all_gather(normed_rows, "vocab", axis=0, tiled=True)
-    raw_keys = jnp.dot(key_rows, key_weight, preferred_element_type=jnp.float32)
-    key_heads = rms_rows(raw_keys, key_gain).astype(jnp.bfloat16)
-
     gate_val = jnp.dot(tokens_in, w_gate[0], preferred_element_type=jnp.float32)
     up_val = jnp.dot(tokens_in, w_up[0], preferred_element_type=jnp.float32)
     hidden = (jax.nn.silu(gate_val) * up_val).astype(jnp.bfloat16)
     parts = jnp.dot(hidden, w_down[0], preferred_element_type=jnp.float32)
     weighted = (parts * my_share).astype(jnp.bfloat16)
+    weighted, key_rows = lax.optimization_barrier((weighted, key_rows))
+    raw_keys = jnp.dot(key_rows, key_weight, preferred_element_type=jnp.float32)
+    key_heads = rms_rows(raw_keys, key_gain).astype(jnp.bfloat16)
     by_tokens = lax.psum_scatter(weighted, "expert", scatter_dimension=0, tiled=True)
     expert_out = lax.psum_scatter(by_tokens, "vocab", scatter_dimension=1, tiled=True)
     return (expert_out, key_heads)

time: 325 us -> 296 us (0.911)
  blocking collectives: 45 us -> 27.9 us
  waiting for transfers between devices: 204 us -> 194 us
    all_gather x1, waiting for transfers between devices: 29.3 us -> 0.01 us  [on_device(): key_rows = lax.all_gather(normed_rows, 'vocab', axis=0, tiled=True)]
    all_to_all x1 -> x0, blocking collectives: 17 us -> none  [on_device(): lax.all_to_all(attn_out, 'vocab', split_axis=0, concat_axis=1, tiled=True)]
    reduce_scatter x1, waiting for transfers between devices: 12.6 us -> 24.4 us  [on_device(): lax.psum_scatter(moved_rows, 'vocab', scatter_dimension=0, tiled=True)]
    reduce_scatter x1, waiting for transfers between devices: 69.4 us -> 72.8 us  [on_device(): lax.psum_scatter(weighted, 'expert', scatter_dimension=0, tiled=True)]
    gather x2 -> x1, local copies, waits for them, and re-layouts: 13.7 us -> 13.3 us  [on_device(): embed_table[safe_ids]]
  transfers between devices with their start and end apart: 5 -> 6, of which waited for: 5 -> 4; matrix products, arithmetic and copies ran while one was open for 1% -> 18% of each run, Pallas kernels for 0% -> 0%
where the time goes in v2:
time: 296 us; the launch traced here: 292 us
  waiting for transfers between devices  194 us (66%)
  matrix products  30.4 us (10%)
  blocking collectives  27.9 us (9%)
  local copies, waits for them, and re-layouts  21.1 us (7%)
  between operations  14.4 us (5%)
  other arithmetic  4.34 us (1%)
    reduce_scatter x1, waiting for transfers between devices, on_device(): lax.psum_scatter(weighted, 'expert', scatter_dimension=0, tiled=True)  72.8 us
    all_gather x1, waiting for transfers between devices, on_device(): tokens_in = lax.all_gather(expert_in, whole_mesh, axis=0, tiled=True)  69.1 us
    reduce_scatter x1, waiting for transfers between devices, on_device(): lax.psum_scatter(by_tokens, 'vocab', scatter_dimension=1, tiled=True)  26.4 us
    reduce_scatter x1, waiting for transfers between devices, on_device(): lax.psum_scatter(moved_rows, 'vocab', scatter_dimension=0, tiled=True)  24.4 us
    all_to_all x1, blocking collectives, on_device(): lax.all_to_all(partial_value, 'expert', split_axis=0, concat_axis=1, tile...  18.9 us
    gather x1, local copies, waits for them, and re-layouts, on_device(): embed_table[safe_ids]  13.3 us
    dot_general x1, matrix products, on_device(): up_val = jnp.dot(tokens_in, w_up[0], preferred_element_type=jnp.float32)  11 us
    dot_general x1, matrix products, on_device(): gate_val = jnp.dot(tokens_in, w_gate[0], preferred_element_type=jnp.float32)  9.95 us
  transfers between devices with their start and end apart: 6, of which 4 were waited for; matrix products, arithmetic and copies ran while one was open for 18% of the time, Pallas kernels for 0%

profile of v2, /device:TPU:8, one launch (start us, length us, event | category | flops | bytes accessed | tf_op | source)
XLA Modules:
  0.0 292.2 jit_solution(1607068945751043418)
XLA Ops:
  7.2 0.7 all-gather.4.cloned.1.call-update
  8.0 0.7 fusion.14
  8.7 5.9 %gather_fusion = s32[1024]{0:T(1024)S(1)} fusion(s32[18992]{0:T(1024)} %param.14, s32[1024]{0:T(1024)S(1)} %fusion.14), kind=kCustom, calls=%fused_computation | custom fusion | bytes 12288 | tf_op jit(solution)/shard_map/gather | solution.py:50
  14.6 13.3 %gather_fusion.1 = bf16[1024,512]{1,0:T(8,128)(2,1)S(1)} fusion(bf16[18992,512]{1,0:T(8,128)(2,1)} %param.15, s32[1024]{0:T(1024)S(1)} %fusion.14), kind=kCustom, calls=%fused_computation.1 | custom fusion | bytes 2101248 | tf_op jit(solution)/shard_map/gather | solution.py:52
  28.0 0.2 broadcast_select_fusion
  28.2 18.9 %all_to_all.16 = bf16[8,128,512]{2,1,0:T(8,128)(2,1)S(1)} all-to-all(bf16[8,128,512]{2,1,0:T(8,128)(2,1)S(1)} %broadcast_select_fusion), channel_id=1, replica_groups=mesh['vocab'=4,'expert'=8] {'expert'}, dimensions={0} | all-to-all | bytes 2097152 | tf_op jit(solution)/shard_map/all_to_all | solution.py:54
  47.1 1.1 copy.25
  48.2 0.0 all-gather.6.cloned.1.call-start
  48.3 24.4 %reduce-scatter.4.cloned.1.call-done = bf16[32,4096]{1,0:T(8,128)(2,1)} async-done(((bf16[128,4096]{1,0:T(8,128)(2,1)}), bf16[32,4096]{1,0:T(8,128)(2,1)}) %reduce-scatter.4.cloned.1.call-update) | async-done | bytes 262160 | tf_op jit(solution)/shard_map/reduce_scatter | solution.py:55
  72.7 1.3 fusion.11
  74.0 2.0 fusion.13
  76.1 0.0 all-gather.8.cloned.1.call-start
  76.2 9.0 %all_gather.14 = f32[1024,16]{0,1:T(8,128)S(1)} all-gather(f32[128,16]{0,1:T(8,128)S(1)} %select_reduce_fusion), channel_id=1, replica_groups=mesh['vocab'=4,'expert'=8] {'expert'}, dimensions={0}, use_global_device_ids=true | all-gather | bytes 73728 | tf_op jit(solution)/shard_map/all_gather | solution.py:40
  85.3 69.1 %all-gather.6.cloned.1.call-done = bf16[1024,4096]{1,0:T(8,128)(2,1)} async-done(((bf16[32,4096]{1,0:T(8,128)(2,1)}), bf16[1024,4096]{1,0:T(8,128)(2,1)}) %all-gather.6.cloned.1.call-update) | async-done | bytes 8388624 | tf_op jit(solution)/shard_map/all_gather | solution.py:60
  154.4 0.2 reduce-scatter.6.cloned.1.call-start
  154.6 11.0 %fusion.1 = f32[1024,768]{1,0:T(8,128)S(1)} fusion(bf16[1024,4096]{1,0:T(8,128)(2,1)} %all-gather.6.cloned.1.call-done, bf16[1,4096,768]{2,1,0:T(8,128)(2,1)} %param.24), kind=kOutput, calls=%fused_computation.4 | convolution fusion | flops 6442450944 | bytes 17825792 | tf_op jit(solution)/shard_map/dot_general | solution.py:66
  165.7 10.0 %multiply_convert_fusion.1 = bf16[1024,768]{1,0:T(8,128)(2,1)S(1)} fusion(f32[1024,768]{1,0:T(8,128)S(1)} %fusion.1, bf16[1024,4096]{1,0:T(8,128)(2,1)S(1)} %copy-done.8, bf16[1,4096,768]{2,1,0:T(8,128)(2,1)} %param.23), kind=kOutput, calls=%fused_computation.8 | convolution fusion | flops 6447169536 | bytes 19398656 | tf_op jit(solution)/shard_map/dot_general | solution.py:65
  175.7 8.9 %multiply_convert_fusion = bf16[1024,4096]{1,0:T(8,128)(2,1)} fusion(f32[1024]{0:T(1024)S(1)} %bitcast.26, bf16[1024,768]{1,0:T(8,128)(2,1)S(1)} %multiply_convert_fusion.1, bf16[1,768,4096]{2,1,0:T(8,128)(2,1)S(1)} %bitcast.28), kind=kOutput, calls=%fused_computation.2 | convolution fusion | flops 6450839552 | bytes 16257024 | tf_op jit(solution)/shard_map/dot_general | solution.py:68
  184.6 0.0 reduce-scatter.8.cloned.1.call-start
  184.7 72.8 %reduce-scatter.6.cloned.1.call-done = bf16[128,4096]{1,0:T(8,128)(2,1)} async-done(((bf16[1024,4096]{1,0:T(8,128)(2,1)}), bf16[128,4096]{1,0:T(8,128)(2,1)}) %reduce-scatter.6.cloned.1.call-update) | async-done | bytes 1048592 | tf_op jit(solution)/shard_map/reduce_scatter | solution.py:73
  257.5 0.6 multiply_reduce_fusion
  258.1 0.1 multiply_convert_fusion.2
  258.2 0.7 copy.24
  258.9 26.4 %reduce-scatter.8.cloned.1.call-done = bf16[128,1024]{1,0:T(8,128)(2,1)} async-done(((bf16[128,4096]{1,0:T(8,128)(2,1)}), bf16[128,1024]{1,0:T(8,128)(2,1)}) %reduce-scatter.8.cloned.1.call-update) | async-done | bytes 262160 | tf_op jit(solution)/shard_map/reduce_scatter | solution.py:74
  (40 shorter events, 0.3 us)
Async XLA Ops:
  7.2 250.3 %copy-start = (bf16[4096,128]{1,0:T(8,128)(2,1)S(1)}, bf16[4096,128]{1,0:T(8,128)(2,1)}, u32[]{:S(2)}) copy-start(bf16[4096,128]{1,0:T(8,128)(2,1)} %param.18) | copy-start | bytes 3145732
  7.2 41.1 %all-gather.4.cloned.1.call-start = ((), (), s32[]{:S(2)}) async-start(), calls=%async_computation.5 | async-start | bytes 1310720 | tf_op jit(solution)/shard_map/all_gather | solution.py:44
  7.9 64.8 %reduce-scatter.4.cloned.1.call-start = ((), (), s32[]{:S(2)}) async-start(), calls=%async_computation.4 | async-start | bytes 1310720 | tf_op jit(solution)/shard_map/reduce_scatter | solution.py:55
  8.7 19.2 %copy-start.5 = (s32[1024]{0:T(1024)S(1)}, s32[1024]{0:T(1024)}, u32[]{:S(2)}) copy-start(s32[1024]{0:T(1024)} %param.13) | copy-start | bytes 12292
  27.9 46.1 %copy-start.2 = (f32[4096]{0:T(1024)S(1)}, f32[4096]{0:T(1024)}, u32[]{:S(2)}) copy-start(f32[4096]{0:T(1024)} %param.17) | copy-start | bytes 49156
  27.9 46.1 %copy-start.3 = (f32[4096]{0:T(1024)S(1)}, f32[4096]{0:T(1024)}, u32[]{:S(2)}) copy-start(f32[4096]{0:T(1024)} %param.20) | copy-start | bytes 49156
  27.9 48.2 %copy-start.4 = (s32[128,8]{0,1:T(8,128)S(1)}, s32[128,8]{0,1:T(8,128)}, u32[]{:S(2)}) copy-start(s32[128,8]{0,1:T(8,128)} %param.22) | copy-start | bytes 12292
  28.0 48.2 %copy-start.6 = (s32[128,8]{0,1:T(8,128)S(1)}, s32[128,8]{0,1:T(8,128)}, u32[]{:S(2)}) copy-start(s32[128,8]{0,1:T(8,128)} %param.21) | copy-start | bytes 12292
  48.2 106.1 %all-gather.6.cloned.1.call-start = ((), (), s32[]{:S(2)}) async-start(), calls=%async_computation.6 | async-start | bytes 8650752 | tf_op jit(solution)/shard_map/all_gather | solution.py:60
  76.1 108.5 %all-gather.8.cloned.1.call-start = ((), (), s32[]{:S(2)}) async-start(), calls=%async_computation.7 | async-start | bytes 1310720 | tf_op jit(solution)/shard_map/all_gather | solution.py:64
  154.4 103.1 %reduce-scatter.6.cloned.1.call-start = ((), (), s32[]{:S(2)}) async-start(), calls=%async_computation.8 | async-start | bytes 9437184 | tf_op jit(solution)/shard_map/reduce_scatter | solution.py:73
  154.6 11.1 %copy-start.8 = (bf16[1024,4096]{1,0:T(8,128)(2,1)S(1)}, bf16[1024,4096]{1,0:T(8,128)(2,1)}, u32[]{:S(2)}) copy-start(bf16[1024,4096]{1,0:T(8,128)(2,1)} %all-gather.6.cloned.1.call-done) | copy-start | bytes 25165828
  154.6 21.1 %slice-start = ((s8[6291456]{0:T(1024)(128)(4,1)}), s8[4194304]{0:T(1024)(128)(4,1)S(1)}, s32[]{:S(2)}) async-start(s8[6291456]{0:T(1024)(128)(4,1)} %bitcast.27), calls=%async_computation.10 | async-start | bytes 8388608
  165.7 10.0 %slice-start.1 = ((s8[6291456]{0:T(1024)(128)(4,1)}), s8[2097152]{0:T(1024)(128)(4,1)S(1)}, s32[]{:S(2)}) async-start(s8[6291456]{0:T(1024)(128)(4,1)} %bitcast.27), calls=%async_computation.11 | async-start | bytes 4194304
  184.6 73.5 %copy-start.7 = (f32[128]{0:T(128)S(1)}, f32[128]{0:T(128)}, u32[]{:S(2)}) copy-start(f32[128]{0:T(128)} %param.19) | copy-start | bytes 1540
  184.6 72.9 %copy-start.1 = (bf16[128,4096]{1,0:T(8,128)(2,1)S(1)}, bf16[128,4096]{1,0:T(8,128)(2,1)}, u32[]{:S(2)}) copy-start(bf16[128,4096]{1,0:T(8,128)(2,1)} %all-gather.8.cloned.1.call-done) | copy-start | bytes 3145732
  184.6 100.7 %reduce-scatter.8.cloned.1.call-start = ((), (), s32[]{:S(2)}) async-start(), calls=%async_computation.9 | async-start | bytes 1310720 | tf_op jit(solution)/shard_map/reduce_scatter | solution.py:74
Sparse Core Ops, SparseCore 0:
  9.6 29.0 all-gather.3
  48.3 24.3 reduce-scatter.3
  76.2 78.1 all-gather.5
  156.4 26.4 all-gather.7
  186.6 70.8 reduce-scatter.5
  260.2 25.0 reduce-scatter.7

commit v3 on v1

--- a/solution.py
+++ b/solution.py
@@ -1,12 +1,227 @@
 import jax
 import jax.numpy as jnp
 from jax import lax
+from jax.experimental import pallas as pl
+from jax.experimental.pallas import tpu as pltpu
 from jax.sharding import PartitionSpec as P
 
 
 def rms_rows(values, scale_gain):
     inverse_rms = lax.rsqrt(jnp.mean(values * values, axis=-1, keepdims=True) + 1e-06)
     return values * inverse_rms * scale_gain
+
+
+def greet(peers):
+    barrier = pltpu.get_barrier_semaphore()
+    for peer in peers:
+        pl.semaphore_signal(barrier, inc=1, device_id=peer, device_id_type=pl.DeviceIdType.MESH)
+    pl.semaphore_wait(barrier, len(peers))
+
+
+def peers_of(n_vocab):
+    me = lax.axis_index("expert")
+    z = lax.axis_index("vocab")
+    core, x, y = me % 2, (me // 2) % 2, me // 4
+    sib, xn, yn = me + 1 - 2 * core, me + 2 - 4 * x, me + 4 - 8 * y
+    along_z = [(z + d) % n_vocab for d in range(1, n_vocab)]
+    ids = [{"expert": sib}, {"expert": xn}, {"expert": yn}] + [{"vocab": p} for p in along_z]
+    return me, z, core, x, y, sib, xn, yn, along_z, ids
+
+
+def add_rows(dst, terms):
+    def step(i, carry):
+        rows = pl.ds(pl.multiple_of(i * 16, 16), 16)
+        total = terms[0][rows, :].astype(jnp.float32)
+        for term in terms[1:]:
+            total = total + term[rows, :].astype(jnp.float32)
+        dst[rows, :] = total.astype(dst.dtype)
+        return carry
+
+    lax.fori_loop(0, dst.shape[0] // 16, step, 0)
+
+
+def reduce_kernel(n_vocab, w, out, core_in, mine, held, a_in, b_in, a_last, b_last, full, z_in,
+                  send, recv, local):
+    me, z, core, x, y, sib, xn, yn, along_z, ids = peers_of(n_vocab)
+    greet(ids)
+    to_sib, to_x, to_y = ids[:3]
+    chunk = [(1 - y) * 2 + 1 - x, y * 2 + 1 - x, (1 - y) * 2 + x, y * 2 + x]
+
+    def move(src, dst, at, peer):
+        return pltpu.make_async_remote_copy(
+            src_ref=src, dst_ref=dst, send_sem=send.at[at], recv_sem=recv.at[at],
+            device_id=peer, device_id_type=pl.DeviceIdType.MESH)
+
+    core_moves = [move(w.at[chunk[r], 1 - core], core_in.at[r], r, to_sib) for r in range(4)]
+    own = [pltpu.make_async_copy(w.at[chunk[r], core], mine.at[r], local.at[r]) for r in range(4)]
+    for r in range(4):
+        core_moves[r].start()
+        own[r].start()
+    a_moves = [move(held.at[0, 0], a_in.at[0], 4, to_x), move(held.at[1, 0], a_in.at[1], 5, to_x)]
+    b_moves = [move(held.at[0, 1], b_in.at[0], 6, to_y), move(held.at[2, 1], b_in.at[1], 7, to_y)]
+    a_then = move(held.at[2, 0], a_last, 8, to_y)
+    b_then = move(held.at[1, 1], b_last, 9, to_x)
+    half = held.shape[3]
+    for r in range(4):
+        own[r].wait()
+        core_moves[r].wait_recv()
+        for h in range(2):
+            columns = pl.ds(h * half, half)
+            add_rows(held.at[r, h], [mine.at[r, :, columns], core_in.at[r, :, columns]])
+        if r == 0:
+            a_moves[0].start()
+            b_moves[0].start()
+        if r == 1:
+            a_moves[1].start()
+        if r == 2:
+            b_moves[1].start()
+    a_moves[0].wait_recv()
+    add_rows(held.at[2, 0], [held.at[2, 0], a_in.at[0]])
+    a_then.start()
+    b_moves[0].wait_recv()
+    add_rows(held.at[1, 1], [held.at[1, 1], b_in.at[0]])
+    b_then.start()
+    quarter = full.shape[2]
+    per_half = half // quarter
+    for moves, then, came, last, h in ((a_moves, a_then, a_in, a_last, 0),
+                                       (b_moves, b_then, b_in, b_last, 1)):
+        moves[1].wait_recv()
+        then.wait_recv()
+        for q in range(per_half):
+            columns = pl.ds(q * quarter, quarter)
+            add_rows(full.at[h * per_half + q],
+                     [held.at[3, h, :, columns], came.at[1, :, columns], last.at[:, columns]])
+    z_moves = [move(full.at[along_z[d]], z_in.at[d], 10 + d, {"vocab": along_z[d]})
+               for d in range(n_vocab - 1)]
+    for moved in z_moves:
+        moved.start()
+    for moved in z_moves:
+        moved.wait_recv()
+    add_rows(out, [full.at[z]] + [z_in.at[d] for d in range(n_vocab - 1)])
+    for moved in core_moves + a_moves + b_moves + [a_then, b_then] + z_moves:
+        moved.wait_send()
+
+
+def reduce_to_owners(weighted, n_vocab):
+    tokens, width = weighted.shape
+    rows, half, quarter = tokens // 8, width // 2, width // n_vocab
+    kind = weighted.dtype
+    return pl.pallas_call(
+        lambda *refs: reduce_kernel(n_vocab, *refs),
+        name="reduce_to_owners",
+        out_shape=jax.ShapeDtypeStruct((rows, quarter), kind),
+        in_specs=[pl.BlockSpec(memory_space=pl.ANY)],
+        out_specs=pl.BlockSpec(memory_space=pltpu.VMEM),
+        scratch_shapes=[
+            pltpu.VMEM((4, rows, width), kind),
+            pltpu.VMEM((4, rows, width), kind),
+            pltpu.VMEM((4, 2, rows, half), kind),
+            pltpu.VMEM((2, rows, half), kind),
+            pltpu.VMEM((2, rows, half), kind),
+            pltpu.VMEM((rows, half), kind),
+            pltpu.VMEM((rows, half), kind),
+            pltpu.VMEM((n_vocab, rows, quarter), kind),
+            pltpu.VMEM((n_vocab - 1, rows, quarter), kind),
+            pltpu.SemaphoreType.DMA((9 + n_vocab,)),
+            pltpu.SemaphoreType.DMA((9 + n_vocab,)),
+            pltpu.SemaphoreType.DMA((4,)),
+        ],
+        compiler_params=pltpu.CompilerParams(
+            collective_id=0, has_side_effects=True, vmem_limit_bytes=40 * 1024 * 1024),
+    )(weighted.reshape(4, 2, rows, width))
+
+
+def gather_kernel(n_vocab, rows_in, keys_in, every, keys, send, recv, local):
+    me, z, core, x, y, sib, xn, yn, along_z, ids = peers_of(n_vocab)
+    greet(ids)
+    to_sib, to_x, to_y = ids[:3]
+    across = xn + 4 - 8 * y
+    started = []
+
+    def move(src, dst, at, peer):
+        return pltpu.make_async_remote_copy(
+            src_ref=src, dst_ref=dst, send_sem=send.at[at], recv_sem=recv.at[at],
+            device_id=peer, device_id_type=pl.DeviceIdType.MESH)
+
+    def begin(src, dst, at, peer):
+        moved = move(src, dst, at, peer)
+        moved.start()
+        started.append(moved)
+
+    def arrived(ref, at):
+        move(ref, ref, at, to_sib).wait_recv()
+
+    far = n_vocab - 1
+    base = 2 * far
+
+    def number(kind, d):
+        return base + kind * n_vocab + d
+
+    for d in range(1, n_vocab):
+        begin(rows_in, every.at[me, z], d - 1, {"vocab": along_z[d - 1]})
+    own_rows = pltpu.make_async_copy(rows_in, every.at[me, z], local.at[0])
+    own_keys = pltpu.make_async_copy(keys_in, keys.at[z], local.at[1])
+    own_rows.start()
+    own_keys.start()
+    origin = [(z - d + n_vocab) % n_vocab for d in range(n_vocab)]
+    for d in range(n_vocab):
+        if d:
+            arrived(every.at[me, origin[d]], d - 1)
+        src = every.at[me, origin[d]] if d else rows_in
+        begin(src, every.at[me, origin[d]], number(0, d), to_x)
+        begin(src, every.at[me, origin[d]], number(1, d), to_y)
+        begin(src, every.at[me, origin[d]], number(2, d), to_sib)
+        if d == 0:
+            for far_d in range(1, n_vocab):
+                begin(keys_in, keys.at[z], far + far_d - 1, {"vocab": along_z[far_d - 1]})
+    for d in range(n_vocab):
+        arrived(every.at[xn, origin[d]], number(0, d))
+        begin(every.at[xn, origin[d], 0], every.at[xn, origin[d], 0], number(3, d), to_y)
+        begin(every.at[xn, origin[d]], every.at[xn, origin[d]], number(4, d), to_sib)
+        arrived(every.at[yn, origin[d]], number(1, d))
+        begin(every.at[yn, origin[d], 1], every.at[yn, origin[d], 1], number(5, d), to_x)
+        begin(every.at[yn, origin[d]], every.at[yn, origin[d]], number(6, d), to_sib)
+    for d in range(n_vocab):
+        for h, kind in ((0, 3), (1, 5)):
+            piece = every.at[across, origin[d], h]
+            arrived(piece, number(kind, d))
+            begin(piece, piece, number(7 + h, d), to_sib)
+    sib_x, sib_y, sib_across = sib + 2 - 4 * x, sib + 4 - 8 * y, sib + 2 - 4 * x + 4 - 8 * y
+    for d in range(n_vocab):
+        arrived(every.at[sib, origin[d]], number(2, d))
+        arrived(every.at[sib_x, origin[d]], number(4, d))
+        arrived(every.at[sib_y, origin[d]], number(6, d))
+        for h in range(2):
+            arrived(every.at[sib_across, origin[d], h], number(7 + h, d))
+        if d:
+            arrived(keys.at[origin[d]], far + d - 1)
+    own_rows.wait()
+    own_keys.wait()
+    for moved in started:
+        moved.wait_send()
+
+
+def gather_rows(expert_in, normed_rows, n_vocab):
+    rows, width = expert_in.shape
+    kind = expert_in.dtype
+    count = 2 * (n_vocab - 1) + 9 * n_vocab
+    every, keys = pl.pallas_call(
+        lambda *refs: gather_kernel(n_vocab, *refs),
+        name="gather_rows",
+        out_shape=(
+            jax.ShapeDtypeStruct((8, n_vocab, 2, rows // 2, width), kind),
+            jax.ShapeDtypeStruct((n_vocab, rows, width), kind),
+        ),
+        in_specs=[pl.BlockSpec(memory_space=pl.ANY)] * 2,
+        out_specs=(pl.BlockSpec(memory_space=pl.ANY), pl.BlockSpec(memory_space=pl.ANY)),
+        scratch_shapes=[
+            pltpu.SemaphoreType.DMA((count,)),
+            pltpu.SemaphoreType.DMA((count,)),
+            pltpu.SemaphoreType.DMA((2,)),
+        ],
+        compiler_params=pltpu.CompilerParams(collective_id=1, has_side_effects=True),
+    )(expert_in.reshape(2, rows // 2, width), normed_rows)
+    return every.reshape(8 * n_vocab * rows, width), keys.reshape(n_vocab * rows, width)
 
 
 def on_device(
@@ -29,6 +244,7 @@
     vocab_rows = embed_table.shape[0]
     experts_total = n_expert * n_vocab // 2
     whole_mesh = ("expert", "vocab")
+    by_kernel = n_expert == 8
     my_vocab = lax.axis_index("vocab")
     my_expert = (lax.axis_index("expert") * n_vocab + my_vocab) // 2
 
@@ -40,7 +256,9 @@
     all_shares = lax.all_gather(share_of, "expert", axis=0, tiled=True)
     my_share = lax.dynamic_slice_in_dim(all_shares, my_expert, 1, axis=1)
 
-    attn_rows = lax.all_to_all(attn_out, "vocab", split_axis=0, concat_axis=1, tiled=True)
+    own_rows = attn_out.shape[0] // n_vocab
+    attn_full = lax.all_gather(attn_out, "vocab", axis=1, tiled=True)
+    attn_rows = lax.dynamic_slice_in_dim(attn_full, my_vocab * own_rows, own_rows, axis=0)
 
     local_ids = token_ids - my_vocab * vocab_rows
     inside = (local_ids >= 0) & (local_ids < vocab_rows)
@@ -55,10 +273,12 @@
 
     mid_rows = (rows + attn_rows.astype(jnp.float32)).astype(jnp.bfloat16)
     expert_in = rms_rows(mid_rows.astype(jnp.float32), post_gain).astype(jnp.bfloat16)
-    tokens_in = lax.all_gather(expert_in, whole_mesh, axis=0, tiled=True)
-
     normed_rows = rms_rows(rows, in_gain).astype(jnp.bfloat16)
-    key_rows = lax.all_gather(normed_rows, "vocab", axis=0, tiled=True)
+    if by_kernel:
+        tokens_in, key_rows = gather_rows(expert_in, normed_rows, n_vocab)
+    else:
+        tokens_in = lax.all_gather(expert_in, whole_mesh, axis=0, tiled=True)
+        key_rows = lax.all_gather(normed_rows, "vocab", axis=0, tiled=True)
     raw_keys = jnp.dot(key_rows, key_weight, preferred_element_type=jnp.float32)
     key_heads = rms_rows(raw_keys, key_gain).astype(jnp.bfloat16)
 
@@ -67,8 +287,11 @@
     hidden = (jax.nn.silu(gate_val) * up_val).astype(jnp.bfloat16)
     parts = jnp.dot(hidden, w_down[0], preferred_element_type=jnp.float32)
     weighted = (parts * my_share).astype(jnp.bfloat16)
-    by_tokens = lax.psum_scatter(weighted, "expert", scatter_dimension=0, tiled=True)
-    expert_out = lax.psum_scatter(by_tokens, "vocab", scatter_dimension=1, tiled=True)
+    if by_kernel:
+        expert_out = reduce_to_owners(weighted, n_vocab)
+    else:
+        by_tokens = lax.psum_scatter(weighted, "expert", scatter_dimension=0, tiled=True)
+        expert_out = lax.psum_scatter(by_tokens, "vocab", scatter_dimension=1, tiled=True)
     return (expert_out, key_heads)
 
 

time: 325 us -> 239 us (0.74); the launches traced: 321 us -> 239 us
  waiting for transfers between devices: 204 us -> 16.9 us
  Pallas kernels: 0 us -> 124 us
  blocking collectives: 45 us -> 27 us
    pallas_call x0 -> x2, Pallas kernels: none -> 124 us  [the longest x1 65 us: reduce_to_owners(): pl.pallas_call(lambda *refs: reduce_kernel(n_vocab, *refs), name='reduce_...]
    all_gather x2 -> x1, waiting for transfers between devices: 96.3 us -> 0.01 us  [on_device(): attn_full = lax.all_gather(attn_out, 'vocab', axis=1, tiled=True)]
    reduce_scatter x2 -> x0, waiting for transfers between devices: 94.1 us -> none  [the longest x1 69.4 us: on_device(): lax.psum_scatter(weighted, 'expert', scatter_dimension=0, tiled=True)]
    all_to_all x1 -> x0, blocking collectives: 17 us -> none  [on_device(): lax.all_to_all(attn_out, 'vocab', split_axis=0, concat_axis=1, tiled=True)]
    reduce_scatter x1, waiting for transfers between devices: 12.6 us -> 16.2 us  [on_device(): lax.psum_scatter(moved_rows, 'vocab', scatter_dimension=0, tiled=True)]
    gather x2 -> x1, local copies, waits for them, and re-layouts: 13.7 us -> 13.3 us  [on_device(): embed_table[safe_ids]]
  transfers between devices with their start and end apart: 5 -> 2, of which waited for: 5 -> 1; matrix products, arithmetic and copies ran while one was open for 1% -> 9% of each run, Pallas kernels for 0% -> 0%
where the time goes in v3:
time: 239 us
  Pallas kernels  124 us (52%)
  matrix products  30 us (13%)
  blocking collectives  27 us (11%)
  local copies, waits for them, and re-layouts  21.9 us (9%)
  waiting for transfers between devices  16.9 us (7%)
  between operations  14.3 us (6%)
  other arithmetic  4.31 us (2%)
    pallas_call x1, Pallas kernels, reduce_to_owners(): pl.pallas_call(lambda *refs: reduce_kernel(n_vocab, *refs), name='reduce_...  65 us
    pallas_call x1, Pallas kernels, gather_rows(): pl.pallas_call(lambda *refs: gather_kernel(n_vocab, *refs), name='gather_...  59.4 us
    all_to_all x1, blocking collectives, on_device(): lax.all_to_all(partial_value, 'expert', split_axis=0, concat_axis=1, tile...  18.9 us
    reduce_scatter x1, waiting for transfers between devices, on_device(): lax.psum_scatter(moved_rows, 'vocab', scatter_dimension=0, tiled=True)  16.2 us
    gather x1, local copies, waits for them, and re-layouts, on_device(): embed_table[safe_ids]  13.3 us
    dot_general x1, matrix products, on_device(): up_val = jnp.dot(tokens_in, w_up[0], preferred_element_type=jnp.float32)  11 us
    dot_general x1, matrix products, on_device(): gate_val = jnp.dot(tokens_in, w_gate[0], preferred_element_type=jnp.float32)  9.93 us
    all_gather x1, blocking collectives, on_device(): all_shares = lax.all_gather(share_of, 'expert', axis=0, tiled=True)  8.12 us
  transfers between devices with their start and end apart: 2, of which 1 were waited for; matrix products, arithmetic and copies ran while one was open for 9% of the time, Pallas kernels for 0%

profile of v3, /device:TPU:8, one launch (start us, length us, event | category | flops | bytes accessed | tf_op | source)
XLA Modules:
  0.0 239.0 jit_solution(16014823539162595958)
XLA Ops:
  7.2 0.0 all-gather.2.cloned.1.call-start
  7.2 0.7 all-gather.2.cloned.1.call-update
  7.9 0.0 reduce-scatter.2.cloned.1.call-start
  8.0 0.7 fusion.14
  8.7 5.9 %gather_fusion = s32[1024]{0:T(1024)S(1)} fusion(s32[18992]{0:T(1024)} %param.14, s32[1024]{0:T(1024)S(1)} %fusion.14), kind=kCustom, calls=%fused_computation | custom fusion | bytes 12288 | tf_op jit(solution)/shard_map/gather | solution.py:266
  14.6 13.3 %gather_fusion.1 = bf16[1024,512]{1,0:T(8,128)(2,1)S(1)} fusion(bf16[18992,512]{1,0:T(8,128)(2,1)} %param.15, s32[1024]{0:T(1024)S(1)} %fusion.14), kind=kCustom, calls=%fused_computation.1 | custom fusion | bytes 2101248 | tf_op jit(solution)/shard_map/gather | solution.py:268
  28.0 0.2 broadcast_select_fusion
  28.2 18.9 %all_to_all.16 = bf16[8,128,512]{2,1,0:T(8,128)(2,1)S(1)} all-to-all(bf16[8,128,512]{2,1,0:T(8,128)(2,1)S(1)} %broadcast_select_fusion), channel_id=1, replica_groups=mesh['vocab'=4,'expert'=8] {'expert'}, dimensions={0} | all-to-all | bytes 2097152 | tf_op jit(solution)/shard_map/all_to_all | solution.py:270
  47.1 1.2 copy.30
  48.3 0.0 reduce-scatter.2.cloned.1.call-update
  48.4 8.1 %all_gather.7 = f32[1024,16]{0,1:T(8,128)S(1)} all-gather(f32[128,16]{0,1:T(8,128)S(1)} %select_reduce_fusion), channel_id=1, replica_groups=mesh['vocab'=4,'expert'=8] {'expert'}, dimensions={0}, use_global_device_ids=true | all-gather | bytes 73728 | tf_op jit(solution)/shard_map/all_gather | solution.py:256
  56.5 0.0 all-gather.2.cloned.1.call-done
  56.5 16.2 %reduce-scatter.2.cloned.1.call-done = bf16[32,4096]{1,0:T(8,128)(2,1)} async-done(((bf16[128,4096]{1,0:T(8,128)(2,1)}), bf16[32,4096]{1,0:T(8,128)(2,1)}) %reduce-scatter.2.cloned.1.call-update) | async-done | bytes 262160 | tf_op jit(solution)/shard_map/reduce_scatter | solution.py:271
  72.8 1.3 fusion.11
  74.1 2.0 fusion.13
  76.1 59.4 %gather_rows.1 = (bf16[8,4,2,16,4096]{4,3,2,1,0:T(8,128)(2,1)}, bf16[4,32,4096]{2,1,0:T(8,128)(2,1)}) custom-call(bf16[2,16,4096]{2,1,0:T(8,128)(2,1)} %bitcast.32, bf16[32,4096]{1,0:T(8,128)(2,1)} %get-tuple-element.16.refs_1_), custom_call_target="tpu_custom_call" | custom-call | tf_op jit(solution)/shard_map/gather_rows/pallas_call | solution.py:208
  135.4 1.8 multiply_reduce_fusion
  137.2 0.1 multiply_convert_fusion.2
  137.3 0.7 copy.29
  138.0 11.0 %fusion.1 = f32[1024,768]{1,0:T(8,128)S(1)} fusion(bf16[1024,4096]{1,0:T(8,128)(2,1)} %bitcast.34, bf16[1,4096,768]{2,1,0:T(8,128)(2,1)} %param.24), kind=kOutput, calls=%fused_computation.4 | convolution fusion | flops 6442450944 | bytes 17825792 | tf_op jit(solution)/shard_map/dot_general | solution.py:286
  149.1 9.9 %multiply_convert_fusion.1 = bf16[1024,768]{1,0:T(8,128)(2,1)S(1)} fusion(f32[1024,768]{1,0:T(8,128)S(1)} %fusion.1, bf16[1024,4096]{1,0:T(8,128)(2,1)S(1)} %bitcast.35, bf16[1,4096,768]{2,1,0:T(8,128)(2,1)} %param.23), kind=kOutput, calls=%fused_computation.8 | convolution fusion | flops 6447169536 | bytes 19398656 | tf_op jit(solution)/shard_map/dot_general | solution.py:285
  159.1 7.3 %multiply_convert_fusion = bf16[1024,4096]{1,0:T(8,128)(2,1)S(1)} fusion(f32[1024]{0:T(1024)S(1)} %bitcast.33, bf16[1024,768]{1,0:T(8,128)(2,1)S(1)} %multiply_convert_fusion.1, bf16[1,768,4096]{2,1,0:T(8,128)(2,1)S(1)} %bitcast.37), kind=kOutput, calls=%fused_computation.2 | convolution fusion | flops 6450839552 | bytes 16257024 | tf_op jit(solution)/shard_map/dot_general | solution.py:288
  166.4 65.0 %reduce_to_owners.1 = bf16[128,1024]{1,0:T(8,128)(2,1)S(1)} custom-call(bf16[4,2,128,4096]{3,2,1,0:T(8,128)(2,1)S(1)} %bitcast.27), custom_call_target="tpu_custom_call" | custom-call | tf_op jit(solution)/shard_map/reduce_to_owners/pallas_call | solution.py:109
  231.4 0.7 copy.32
  (31 shorter events, 0.2 us)
Async XLA Ops:
  7.2 128.3 %copy-start = (bf16[4096,128]{1,0:T(8,128)(2,1)S(1)}, bf16[4096,128]{1,0:T(8,128)(2,1)}, u32[]{:S(2)}) copy-start(bf16[4096,128]{1,0:T(8,128)(2,1)} %param.18) | copy-start | bytes 3145732
  7.2 49.4 %all-gather.2.cloned.1.call-start = ((), (), s32[]{:S(2)}) async-start(), calls=%async_computation.3 | async-start | bytes 1310720 | tf_op jit(solution)/shard_map/all_gather | solution.py:260
  7.9 64.9 %reduce-scatter.2.cloned.1.call-start = ((), (), s32[]{:S(2)}) async-start(), calls=%async_computation.2 | async-start | bytes 1310720 | tf_op jit(solution)/shard_map/reduce_scatter | solution.py:271
  8.7 19.3 %copy-start.5 = (s32[1024]{0:T(1024)S(1)}, s32[1024]{0:T(1024)}, u32[]{:S(2)}) copy-start(s32[1024]{0:T(1024)} %param.13) | copy-start | bytes 12292
  14.6 33.7 %copy-start.4 = (s32[128,8]{0,1:T(8,128)S(1)}, s32[128,8]{0,1:T(8,128)}, u32[]{:S(2)}) copy-start(s32[128,8]{0,1:T(8,128)} %param.22) | copy-start | bytes 12292
  14.6 33.7 %copy-start.6 = (s32[128,8]{0,1:T(8,128)S(1)}, s32[128,8]{0,1:T(8,128)}, u32[]{:S(2)}) copy-start(s32[128,8]{0,1:T(8,128)} %param.21) | copy-start | bytes 12292
  28.0 46.1 %copy-start.2 = (f32[4096]{0:T(1024)S(1)}, f32[4096]{0:T(1024)}, u32[]{:S(2)}) copy-start(f32[4096]{0:T(1024)} %param.17) | copy-start | bytes 49156
  28.0 46.1 %copy-start.3 = (f32[4096]{0:T(1024)S(1)}, f32[4096]{0:T(1024)}, u32[]{:S(2)}) copy-start(f32[4096]{0:T(1024)} %param.20) | copy-start | bytes 49156
  28.0 109.2 %copy-start.7 = (f32[128]{0:T(128)S(1)}, f32[128]{0:T(128)}, u32[]{:S(2)}) copy-start(f32[128]{0:T(128)} %param.19) | copy-start | bytes 1540
  138.0 11.0 %copy-start.8 = (bf16[8,4,2,16,4096]{4,3,2,1,0:T(8,128)(2,1)S(1)}, bf16[8,4,2,16,4096]{4,3,2,1,0:T(8,128)(2,1)}, u32[]{:S(2)}) copy-start(bf16[8,4,2,16,4096]{4,3,2,1,0:T(8,128)(2,1)} %get-tuple-element.4) | copy-start | bytes 25165828
  138.0 21.0 %slice-start = ((s8[6291456]{0:T(1024)(128)(4,1)}), s8[4194304]{0:T(1024)(128)(4,1)S(1)}, s32[]{:S(2)}) async-start(s8[6291456]{0:T(1024)(128)(4,1)} %bitcast.36), calls=%async_computation.4 | async-start | bytes 8388608
  149.1 10.0 %slice-start.1 = ((s8[6291456]{0:T(1024)(128)(4,1)}), s8[2097152]{0:T(1024)(128)(4,1)S(1)}, s32[]{:S(2)}) async-start(s8[6291456]{0:T(1024)(128)(4,1)} %bitcast.36), calls=%async_computation.5 | async-start | bytes 4194304
  159.1 73.1 %copy-start.1 = (bf16[4096,128]{1,0:T(8,128)(2,1)S(1)}, bf16[4096,128]{1,0:T(8,128)(2,1)}, u32[]{:S(2)}) copy-start(bf16[4096,128]{1,0:T(8,128)(2,1)} %param.18) | copy-start | bytes 3145732
Sparse Core Ops, SparseCore 0:
  9.6 29.0 all-gather.1
  48.4 24.3 reduce-scatter.1

commit v4 on v3

--- a/solution.py
+++ b/solution.py
@@ -257,18 +257,27 @@
     my_share = lax.dynamic_slice_in_dim(all_shares, my_expert, 1, axis=1)
 
     own_rows = attn_out.shape[0] // n_vocab
-    attn_full = lax.all_gather(attn_out, "vocab", axis=1, tiled=True)
-    attn_rows = lax.dynamic_slice_in_dim(attn_full, my_vocab * own_rows, own_rows, axis=0)
-
-    local_ids = token_ids - my_vocab * vocab_rows
+    attn_blocks = attn_out.reshape(n_vocab, own_rows, attn_out.shape[1])
+    kept = lax.dynamic_index_in_dim(attn_blocks, my_vocab, 0, keepdims=True)
+    attn_parts = lax.dynamic_update_slice_in_dim(attn_blocks, kept, my_vocab, 0)
+    for d in range(1, n_vocab):
+        sent = lax.dynamic_index_in_dim(attn_blocks, (my_vocab + d) % n_vocab, 0, keepdims=True)
+        came = lax.ppermute(sent, "vocab", [(i, (i + d) % n_vocab) for i in range(n_vocab)])
+        attn_parts = lax.dynamic_update_slice_in_dim(
+            attn_parts, came, (my_vocab - d + n_vocab) % n_vocab, 0
+        )
+    attn_rows = attn_parts.transpose(1, 0, 2).reshape(own_rows, -1)
+
+    ids = token_ids.reshape(n_expert, n_vocab, own_rows).transpose(1, 0, 2).reshape(-1)
+    local_ids = ids - my_vocab * vocab_rows
     inside = (local_ids >= 0) & (local_ids < vocab_rows)
     safe_ids = jnp.clip(local_ids, 0, vocab_rows - 1)
     keep_row = inside & (word_mask[safe_ids] == 1)
     partial_value = jnp.where(
         keep_row[:, None], embed_table[safe_ids], jnp.zeros_like(embed_table[:1])
     )
-    moved_rows = lax.all_to_all(partial_value, "expert", split_axis=0, concat_axis=1, tiled=True)
-    rows = lax.psum_scatter(moved_rows, "vocab", scatter_dimension=0, tiled=True)
+    summed = lax.psum_scatter(partial_value, "vocab", scatter_dimension=0, tiled=True)
+    rows = lax.all_to_all(summed, "expert", split_axis=0, concat_axis=1, tiled=True)
     rows = rows.astype(jnp.float32)
 
     mid_rows = (rows + attn_rows.astype(jnp.float32)).astype(jnp.bfloat16)

time: 239 us -> 234 us (0.979)
  blocking collectives: 27 us -> 9.08 us
  starting transfers between devices: 0.08 us -> 8.43 us
  waiting for transfers between devices: 16.9 us -> 21.3 us
  local copies, waits for them, and re-layouts: 21.9 us -> 26.1 us
  matrix products: 30 us -> 27.5 us
    all_to_all x1 -> x0, blocking collectives: 18.9 us -> none  [on_device(): lax.all_to_all(partial_value, 'expert', split_axis=0, concat_axis=1, tile...]
    reduce_scatter x1, waiting for transfers between devices: 16.2 us -> 3.66 us  [on_device(): lax.psum_scatter(partial_value, 'vocab', scatter_dimension=0, tiled=True)]
    ppermute x0 -> x3, waiting for transfers between devices: none -> 11.3 us  [on_device(): lax.ppermute(sent, 'vocab', [(i, (i + d) % n_vocab) for i in range(n_voca...]
    all_to_all x0 -> x1, waiting for transfers between devices: none -> 6.28 us  [on_device(): lax.all_to_all(summed, 'expert', split_axis=0, concat_axis=1, tiled=True)]
    ppermute x0 -> x3, starting transfers between devices: none -> 4.67 us  [on_device(): lax.ppermute(sent, 'vocab', [(i, (i + d) % n_vocab) for i in range(n_voca...]
    all_to_all x0 -> x1, starting transfers between devices: none -> 3.72 us  [on_device(): lax.all_to_all(summed, 'expert', split_axis=0, concat_axis=1, tiled=True)]
    dynamic_update_slice x0 -> x4, local copies, waits for them, and re-layouts: none -> 3.47 us  [the longest x3 2.6 us: on_device(): lax.dynamic_update_slice_in_dim(attn_parts, came, (my_vocab - d + n_vocab...]
    dot_general x1, matrix products: 9.93 us -> 7.01 us  [on_device(): gate_val = jnp.dot(tokens_in, w_gate[0], preferred_element_type=jnp.float32)]
  transfers between devices with their start and end apart: 2 -> 5, of which waited for: 1 -> 4; matrix products, arithmetic and copies ran while one was open for 9% -> 2% of each run, Pallas kernels for 0% -> 0%
where the time goes in v4:
time: 234 us
  Pallas kernels  122 us (52%)
  matrix products  27.5 us (12%)
  local copies, waits for them, and re-layouts  26.1 us (11%)
  waiting for transfers between devices  21.3 us (9%)
  between operations  14.5 us (6%)
  blocking collectives  9.08 us (4%)
  starting transfers between devices  8.43 us (4%)
  other arithmetic  5.05 us (2%)
    pallas_call x1, Pallas kernels, reduce_to_owners(): pl.pallas_call(lambda *refs: reduce_kernel(n_vocab, *refs), name='reduce_...  65 us
    pallas_call x1, Pallas kernels, gather_rows(): pl.pallas_call(lambda *refs: gather_kernel(n_vocab, *refs), name='gather_...  56.8 us
    gather x1, local copies, waits for them, and re-layouts, on_device(): embed_table[safe_ids]  13.1 us
    ppermute x3, waiting for transfers between devices, on_device(): lax.ppermute(sent, 'vocab', [(i, (i + d) % n_vocab) for i in range(n_voca...  11.3 us
    dot_general x1, matrix products, on_device(): up_val = jnp.dot(tokens_in, w_up[0], preferred_element_type=jnp.float32)  11 us
    all_gather x1, blocking collectives, on_device(): all_shares = lax.all_gather(share_of, 'expert', axis=0, tiled=True)  9.08 us
    dot_general x1, matrix products, on_device(): parts = jnp.dot(hidden, w_down[0], preferred_element_type=jnp.float32)  7.54 us
    dot_general x1, matrix products, on_device(): gate_val = jnp.dot(tokens_in, w_gate[0], preferred_element_type=jnp.float32)  7.01 us
  transfers between devices with their start and end apart: 5, of which 4 were waited for; matrix products, arithmetic and copies ran while one was open for 2% of the time, Pallas kernels for 0%

profile of v4, /device:TPU:8, one launch (start us, length us, event | category | flops | bytes accessed | tf_op | source)
XLA Modules:
  0.0 233.8 jit_solution(10370306900909903850)
XLA Ops:
  9.1 5.9 %gather_fusion = s32[1024]{0:T(1024)S(1)} fusion(s32[18992]{0:T(1024)} %param.14, s32[1024]{0:T(1024)S(1)} %broadcast_clamp_fusion), kind=kCustom, calls=%fused_computation | custom fusion | bytes 12288 | tf_op jit(solution)/shard_map/gather | solution.py:275
  15.0 13.1 %gather_fusion.1 = bf16[1024,512]{1,0:T(8,128)(2,1)S(1)} fusion(bf16[18992,512]{1,0:T(8,128)(2,1)} %param.15, s32[1024]{0:T(1024)S(1)} %broadcast_clamp_fusion), kind=kCustom, calls=%fused_computation.1 | custom fusion | bytes 2101248 | tf_op jit(solution)/shard_map/gather | solution.py:277
  28.1 1.2 broadcast_select_fusion
  30.2 1.6 collective-permute-start
  31.8 1.1 collective-permute-start.1
  32.9 1.9 collective-permute-start.2
  34.8 0.9 dynamic_update_slice.12
  35.8 9.1 %all_gather.3 = f32[1024,16]{0,1:T(8,128)S(1)} all-gather(f32[128,16]{0,1:T(8,128)S(1)} %select_reduce_fusion), channel_id=1, replica_groups=mesh['vocab'=4,'expert'=8] {'expert'}, dimensions={0}, use_global_device_ids=true | all-gather | bytes 73728 | tf_op jit(solution)/shard_map/all_gather | solution.py:256
  44.9 0.9 dynamic_update_slice.13
  45.8 6.3 %collective-permute-done.1 = bf16[1,32,1024]{2,0,1:T(2,128)(2,1)S(1)} collective-permute-done((bf16[1,32,1024]{2,0,1:T(2,128)(2,1)S(1)}, bf16[1,32,1024]{2,0,1:T(2,128)(2,1)S(1)}, u32[]{:S(2)}, u32[]{:S(2)}) %collective-permute-start.1) | collective-permute-done | bytes 65568 | tf_op jit(solution)/shard_map/ppermute | solution.py:265
  52.1 0.8 dynamic_update_slice.14
  52.9 5.0 %collective-permute-done.2 = bf16[1,32,1024]{2,0,1:T(2,128)(2,1)S(1)} collective-permute-done((bf16[1,32,1024]{2,0,1:T(2,128)(2,1)S(1)}, bf16[1,32,1024]{2,0,1:T(2,128)(2,1)S(1)}, u32[]{:S(2)}, u32[]{:S(2)}) %collective-permute-start.2) | collective-permute-done | bytes 65568 | tf_op jit(solution)/shard_map/ppermute | solution.py:265
  58.0 0.9 dynamic_update_slice.15
  58.9 3.7 %reduce-scatter.2.cloned.1.call-done = bf16[256,512]{1,0:T(8,128)(2,1)} async-done(((bf16[1024,512]{1,0:T(8,128)(2,1)}), bf16[256,512]{1,0:T(8,128)(2,1)}) %reduce-scatter.2.cloned.1.call-update) | async-done | bytes 262160 | tf_op jit(solution)/shard_map/reduce_scatter | solution.py:279
  62.5 3.7 %all-to-all-start = ((bf16[8,32,512]{2,1,0:T(8,128)(2,1)}), bf16[8,32,512]{2,1,0:T(8,128)(2,1)S(1)}, u32[]{:S(2)}, u32[]{:S(2)}) async-start(bf16[8,32,512]{2,1,0:T(8,128)(2,1)} %bitcast.40), calls=%async_computation.1 | async-start | bytes 524288 | tf_op jit(solution)/shard_map/all_to_all | solution.py:280
  66.9 6.3 %all-to-all-done = bf16[8,32,512]{2,1,0:T(8,128)(2,1)S(1)} async-done(((bf16[8,32,512]{2,1,0:T(8,128)(2,1)}), bf16[8,32,512]{2,1,0:T(8,128)(2,1)S(1)}, u32[]{:S(2)}, u32[]{:S(2)}) %all-to-all-start) | async-done | bytes 262176 | tf_op jit(solution)/shard_map/all_to_all | solution.py:280
  74.3 0.8 multiply_convert_fusion.2.refs_1_
  75.1 0.8 multiply_convert_fusion.3.refs_0_
  75.9 56.8 %gather_rows.1 = (bf16[8,4,2,16,4096]{4,3,2,1,0:T(8,128)(2,1)}, bf16[4,32,4096]{2,1,0:T(8,128)(2,1)}) custom-call(bf16[2,16,4096]{2,1,0:T(8,128)(2,1)} %multiply_convert_fusion.3.refs_0_, bf16[32,4096]{1,0:T(8,128)(2,1)} %multiply_convert_fusion.2.refs_1_), custom_call_target="tpu_custom_call" | custom-call | tf_op jit(solution)/shard_map/gather_rows/pallas_call | solution.py:208
  132.8 1.9 multiply_reduce_fusion.2
  135.5 11.0 %fusion.1 = f32[1024,768]{1,0:T(8,128)S(1)} fusion(bf16[1024,4096]{1,0:T(8,128)(2,1)} %bitcast.45, bf16[1,4096,768]{2,1,0:T(8,128)(2,1)} %param.24), kind=kOutput, calls=%fused_computation.4 | convolution fusion | flops 6442450944 | bytes 17825792 | tf_op jit(solution)/shard_map/dot_general | solution.py:295
  146.6 7.0 %multiply_convert_fusion.1 = bf16[1024,768]{1,0:T(8,128)(2,1)S(1)} fusion(f32[1024,768]{1,0:T(8,128)S(1)} %fusion.1, bf16[1024,4096]{1,0:T(8,128)(2,1)S(1)} %bitcast.46, bf16[1,4096,768]{2,1,0:T(8,128)(2,1)S(1)} %bitcast.48), kind=kOutput, calls=%fused_computation.8 | convolution fusion | flops 6447169536 | bytes 19398656 | tf_op jit(solution)/shard_map/dot_general | solution.py:294
  153.7 7.5 %multiply_convert_fusion = bf16[1024,4096]{1,0:T(8,128)(2,1)S(1)} fusion(f32[1024]{0:T(1024)S(1)} %bitcast.44, bf16[1024,768]{1,0:T(8,128)(2,1)S(1)} %multiply_convert_fusion.1, bf16[1,768,4096]{2,1,0:T(8,128)(2,1)S(1)} %bitcast.50), kind=kOutput, calls=%fused_computation.2 | convolution fusion | flops 6450839552 | bytes 16257024 | tf_op jit(solution)/shard_map/dot_general | solution.py:297
  161.2 65.0 %reduce_to_owners.1 = bf16[128,1024]{1,0:T(8,128)(2,1)S(1)} custom-call(bf16[4,2,128,4096]{3,2,1,0:T(8,128)(2,1)S(1)} %bitcast.35), custom_call_target="tpu_custom_call" | custom-call | tf_op jit(solution)/shard_map/reduce_to_owners/pallas_call | solution.py:109
  (62 shorter events, 6.0 us)
Async XLA Ops:
  7.2 125.6 %copy-start = (bf16[4096,128]{1,0:T(8,128)(2,1)S(1)}, bf16[4096,128]{1,0:T(8,128)(2,1)}, u32[]{:S(2)}) copy-start(bf16[4096,128]{1,0:T(8,128)(2,1)} %param.18) | copy-start | bytes 3145732
  7.2 55.3 %reduce-scatter.2.cloned.1.call-start = ((), (), s32[]{:S(2)}) async-start(), calls=%async_computation.2 | async-start | bytes 1310720 | tf_op jit(solution)/shard_map/reduce_scatter | solution.py:279
  15.0 14.4 %copy-start.2 = (bf16[128,1024]{1,0:T(8,128)(2,1)S(1)}, bf16[128,1024]{1,0:T(8,128)(2,1)}, u32[]{:S(2)}) copy-start(bf16[128,1024]{1,0:T(8,128)(2,1)} %param.16) | copy-start | bytes 786436
  15.0 20.7 %copy-start.5 = (s32[128,8]{0,1:T(8,128)S(1)}, s32[128,8]{0,1:T(8,128)}, u32[]{:S(2)}) copy-start(s32[128,8]{0,1:T(8,128)} %param.22) | copy-start | bytes 12292
  15.0 20.8 %copy-start.6 = (s32[128,8]{0,1:T(8,128)S(1)}, s32[128,8]{0,1:T(8,128)}, u32[]{:S(2)}) copy-start(s32[128,8]{0,1:T(8,128)} %param.21) | copy-start | bytes 12292
  29.3 45.0 %copy-start.4 = (f32[4096]{0:T(1024)S(1)}, f32[4096]{0:T(1024)}, u32[]{:S(2)}) copy-start(f32[4096]{0:T(1024)} %param.17) | copy-start | bytes 49156
  29.3 45.8 %copy-start.3 = (f32[4096]{0:T(1024)S(1)}, f32[4096]{0:T(1024)}, u32[]{:S(2)}) copy-start(f32[4096]{0:T(1024)} %param.20) | copy-start | bytes 49156
  30.2 14.7 %collective-permute-start = (bf16[1,32,1024]{2,0,1:T(2,128)(2,1)S(1)}, bf16[1,32,1024]{2,0,1:T(2,128)(2,1)S(1)}, u32[]{:S(2)}, u32[]{:S(2)}) collective-permute-start(bf16[1,32,1024]{2,0,1:T(2,128)(2,1)S(1)} %get-tuple-element.24), channel_id=1, source_target_pairs={{0,8},{8,16},{16,24},{24,0},{1,9},{9,17},{17,25},{25,1},{2,10},{10... | collective-permute-start | bytes 196616 | tf_op jit(solution)/shard_map/ppermute | solution.py:265
  31.8 20.3 %collective-permute-start.1 = (bf16[1,32,1024]{2,0,1:T(2,128)(2,1)S(1)}, bf16[1,32,1024]{2,0,1:T(2,128)(2,1)S(1)}, u32[]{:S(2)}, u32[]{:S(2)}) collective-permute-start(bf16[1,32,1024]{2,0,1:T(2,128)(2,1)S(1)} %get-tuple-element.23), channel_id=1, source_target_pairs={{0,16},{8,24},{16,0},{24,8},{1,17},{9,25},{17,1},{25,9},{2,18},{10... | collective-permute-start | bytes 196616 | tf_op jit(solution)/shard_map/ppermute | solution.py:265
  32.9 25.1 %collective-permute-start.2 = (bf16[1,32,1024]{2,0,1:T(2,128)(2,1)S(1)}, bf16[1,32,1024]{2,0,1:T(2,128)(2,1)S(1)}, u32[]{:S(2)}, u32[]{:S(2)}) collective-permute-start(bf16[1,32,1024]{2,0,1:T(2,128)(2,1)S(1)} %get-tuple-element.22), channel_id=1, source_target_pairs={{0,24},{8,0},{16,8},{24,16},{1,25},{9,1},{17,9},{25,17},{2,26},{10... | collective-permute-start | bytes 196616 | tf_op jit(solution)/shard_map/ppermute | solution.py:265
  58.9 75.8 %copy-start.7 = (f32[128]{0:T(128)S(1)}, f32[128]{0:T(128)}, u32[]{:S(2)}) copy-start(f32[128]{0:T(128)} %param.19) | copy-start | bytes 1540
  62.5 10.7 %all-to-all-start = ((bf16[8,32,512]{2,1,0:T(8,128)(2,1)}), bf16[8,32,512]{2,1,0:T(8,128)(2,1)S(1)}, u32[]{:S(2)}, u32[]{:S(2)}) async-start(bf16[8,32,512]{2,1,0:T(8,128)(2,1)} %bitcast.40), calls=%async_computation.1 | async-start | bytes 524288 | tf_op jit(solution)/shard_map/all_to_all | solution.py:280
  132.7 13.8 %slice-start = ((s8[6291456]{0:T(1024)(128)(4,1)}), s8[2097152]{0:T(1024)(128)(4,1)S(1)}, s32[]{:S(2)}) async-start(s8[6291456]{0:T(1024)(128)(4,1)} %bitcast.47), calls=%async_computation.3 | async-start | bytes 4194304
  135.5 11.1 %copy-start.8 = (bf16[8,4,2,16,4096]{4,3,2,1,0:T(8,128)(2,1)S(1)}, bf16[8,4,2,16,4096]{4,3,2,1,0:T(8,128)(2,1)}, u32[]{:S(2)}) copy-start(bf16[8,4,2,16,4096]{4,3,2,1,0:T(8,128)(2,1)} %get-tuple-element.4) | copy-start | bytes 25165828
  135.5 11.1 %slice-start.1 = ((s8[6291456]{0:T(1024)(128)(4,1)}), s8[4194304]{0:T(1024)(128)(4,1)S(1)}, s32[]{:S(2)}) async-start(s8[6291456]{0:T(1024)(128)(4,1)} %bitcast.47), calls=%async_computation.4 | async-start | bytes 8388608
  135.5 18.1 %slice-start.2 = ((s8[6291456]{0:T(1024)(128)(4,1)}), s8[4194304]{0:T(1024)(128)(4,1)S(1)}, s32[]{:S(2)}) async-start(s8[6291456]{0:T(1024)(128)(4,1)} %bitcast.49), calls=%async_computation.5 | async-start | bytes 8388608
  146.6 7.0 %slice-start.3 = ((s8[6291456]{0:T(1024)(128)(4,1)}), s8[2097152]{0:T(1024)(128)(4,1)S(1)}, s32[]{:S(2)}) async-start(s8[6291456]{0:T(1024)(128)(4,1)} %bitcast.49), calls=%async_computation.6 | async-start | bytes 4194304
  153.6 73.3 %copy-start.1 = (bf16[4096,128]{1,0:T(8,128)(2,1)S(1)}, bf16[4096,128]{1,0:T(8,128)(2,1)}, u32[]{:S(2)}) copy-start(bf16[4096,128]{1,0:T(8,128)(2,1)} %param.18) | copy-start | bytes 3145732
Sparse Core Ops, SparseCore 0:
  29.4 33.0 reduce-scatter.1
